TPU v7x, 256 devices: a whole 4x4x8 slice. The times are simulated.
256 devices in a mesh: section: 2 (over core), wide: 16 (over y, x), narrow: 8 (over z).
Axes of the slice: x: 4, y: 4, z: 8, core: 2. Of those that a mesh axis runs over, the one named last changes fastest.
Arguments:
- hidden_in: bfloat16 [2, 1024, 3072], P(None, 'wide', 'narrow'), may hold values from -64 to 64
- row_kind: int32 [2, 1024], replicated, may hold values from 0 to 3, as said below
- positions: int32 [3, 2, 1024], replicated, may hold values from 0 to 44, as said below
- timesteps: int32 [2], replicated, may hold values from 0 to 999
- stale_cache: bfloat16 [2, 2, 1024, 48, 128], P('section', None, 'narrow', 'wide'), may hold values from -8 to 8
- w_qkv: bfloat16 [2, 3072, 9216], P('section', 'narrow', 'wide'), may hold values from -0.109375 to 0.109375
- qk_norm: float32 [2, 4, 64], P('section'), may hold values from -6 to 6, as said below
- w_out: bfloat16 [2, 3072, 3072], P('section', 'wide', 'narrow'), may hold values from -0.109375 to 0.109375
- ada_weight: bfloat16 [2, 2, 512, 6, 3072], P('section', None, None, None, 'narrow'), may hold values from -0.25 to 0.25
- w_up: bfloat16 [2, 3072, 12288], P('section', 'narrow', 'wide'), may hold values from -0.109375 to 0.109375
- w_down: bfloat16 [2, 12288, 3072], P('section', 'wide', 'narrow'), may hold values from -0.0546875 to 0.0546875
Outputs:
- layer_out: bfloat16 [2, 2, 1024, 3072], P('section', None, 'wide', 'narrow')
- new_cache: bfloat16 [2, 2, 1024, 48, 128], P('section', None, 'narrow', 'wide')
Inputs may be any that keep to these rules, and one draw needn't show every extreme that they name: `row_kind`: kind is 2 times the request (0 or 1) plus 1 for a text row. In each patch the rows of request 0 come first and those of request 1 follow, each request holding 1024/4 rows or more; text rows stand only in patch 0, as the first 128 rows of each request's block. `positions`: rows 0, 1, 2 are frame (below 13), height (below 30) and width (below 45); text rows have all three zero. `qk_norm`: rows are query gain, query bias, key gain, key bias; gains lie in 0.6 to 1.4.
All inputs are finite; a program needn't handle non-finite values.
Results may differ from a plain program's by a relative error of at most 0.019.
Values may be sent and summed in bfloat16 or wider, within the bound.
A program may use at most 128 MiB of HBM per device.

v0:
```python
import jax
import jax.numpy as jnp
from jax import lax
from jax.sharding import PartitionSpec as P

EPS_ROW = 1e-05
EPS_HEAD = 1e-06
NEG_FILL = -1e30


def passed_along(value, axis, by):
    devices = lax.axis_size(axis)
    pairs = [(i, i + by) for i in range(devices) if 0 <= i + by < devices]
    return lax.ppermute(value, axis, pairs)


def time_features(timesteps, feature_count):
    half_count = feature_count // 2
    frequency = jnp.exp(-jnp.log(10000.0) * jnp.arange(half_count, dtype=jnp.float32) / half_count)
    angle = timesteps.astype(jnp.float32)[:, None] * frequency[None, :]
    return jnp.concatenate([jnp.cos(angle), jnp.sin(angle)], axis=1)


def rotary_angles(row_positions, head_dim):
    dim_frame = head_dim // 4
    dim_plane = head_dim // 8 * 3
    pieces = []
    for axis_pos, span_dims in ((0, dim_frame), (1, dim_plane), (2, dim_plane)):
        frequency = 10000.0 ** (-jnp.arange(0, span_dims, 2, dtype=jnp.float32) / span_dims)
        pieces.append(row_positions[axis_pos].astype(jnp.float32)[:, None] * frequency[None, :])
    return jnp.concatenate(pieces, axis=1)


def rotate(values, angles):
    row_count, head_count, head_dim = values.shape
    paired = values.reshape(row_count, head_count, head_dim // 2, 2)
    former = paired[..., 0]
    latter = paired[..., 1]
    cosine = jnp.cos(angles)[:, None, :]
    sine = jnp.sin(angles)[:, None, :]
    turned = jnp.stack([former * cosine - latter * sine, latter * cosine + former * sine], axis=-1)
    return turned.reshape(row_count, head_count, head_dim)


def head_norm(values, gain, offset):
    center = values - jnp.mean(values, axis=-1, keepdims=True)
    spread = jnp.mean(center * center, axis=-1, keepdims=True)
    return center * lax.rsqrt(spread + EPS_HEAD) * gain + offset


def select_rows(table, kinds):
    match = (kinds[:, None] == jnp.arange(4, dtype=jnp.int32)[None, :]).astype(jnp.float32)
    return jnp.sum(match[:, :, None, None] * table[None], axis=1)


def partial_softmax(queries, query_req, keys_flat, key_req, head_dim):
    scores = jnp.einsum(
        "qhd,khd->qhk", queries, keys_flat[..., :head_dim], preferred_element_type=jnp.float32
    )
    scores = scores * head_dim ** (-0.5)
    allowed = (query_req[:, None] == key_req[None, :])[:, None, :]
    masked = jnp.where(allowed, scores, NEG_FILL)
    top = jnp.max(masked, axis=2)
    weights = jnp.where(allowed, jnp.exp(masked - top[..., None]), 0.0)
    total = jnp.sum(weights, axis=2)
    accum = jnp.einsum(
        "qhk,khd->qhd",
        weights.astype(jnp.bfloat16),
        keys_flat[..., head_dim:],
        preferred_element_type=jnp.float32,
    )
    return (top, total, accum)


def combine_parts(former, latter):
    top = jnp.maximum(former[0], latter[0])
    factor_b = jnp.exp(latter[0] - top)
    total = latter[1] * factor_b
    accum = latter[2] * factor_b[..., None]
    return (top, total, accum)


def per_device(
    hidden_in,
    row_kind,
    positions,
    timesteps,
    stale_cache,
    w_qkv,
    qk_norm,
    w_out,
    ada_weight,
    w_up,
    w_down,
):
    n_wide = lax.axis_size("wide")
    n_narrow = lax.axis_size("narrow")
    n_section = lax.axis_size("section")
    wide_idx = lax.axis_index("wide")
    narrow_idx = lax.axis_index("narrow")
    section_idx = lax.axis_index("section")
    patch_count, rows_a, feat_a = hidden_in.shape
    total_rows = rows_a * n_wide
    rows_b = total_rows // n_narrow
    heads_local = stale_cache.shape[3]
    head_dim = stale_cache.shape[4] // 2
    model_width = feat_a * n_narrow
    zero_index = jnp.zeros((), jnp.int32)
    activated = jax.nn.silu(time_features(timesteps, ada_weight.shape[2])).astype(jnp.bfloat16)
    modulation = jnp.einsum(
        "re,kesd->krsd", activated, ada_weight[0], preferred_element_type=jnp.float32
    )
    tables = modulation.reshape(2, 4, 3, feat_a)
    norms = qk_norm[0]
    qkv_block = w_qkv[0]
    out_block = w_out[0]
    up_block = w_up[0]
    down_block = w_down[0]

    def normalize(values):
        moments = lax.psum((jnp.sum(values, axis=1), jnp.sum(values * values, axis=1)), "narrow")
        row_mean = moments[0] / model_width
        variance = moments[1] / model_width - row_mean * row_mean
        return (values - row_mean[:, None]) * lax.rsqrt(variance + EPS_ROW)[:, None]

    outputs = jnp.zeros((1, patch_count, rows_a, feat_a), jnp.bfloat16)
    cache_now = stale_cache
    arriving = jnp.zeros((rows_a, feat_a), jnp.bfloat16)
    step_total = patch_count + n_section - 1
    for step_index in range(step_total):
        patch_index = step_index - section_idx
        is_live = (patch_index >= 0) & (patch_index < patch_count)
        patch_slot = jnp.clip(patch_index, 0, patch_count - 1)
        layer_in = jnp.where(
            section_idx == 0, hidden_in[min(step_index, patch_count - 1)], arriving
        )
        x_in = layer_in.astype(jnp.float32)
        kinds_a = lax.dynamic_slice(row_kind, (patch_slot, wide_idx * rows_a), (1, rows_a))[0]
        kinds_b = lax.dynamic_slice(row_kind, (patch_slot, narrow_idx * rows_b), (1, rows_b))[0]
        positions_b = lax.dynamic_slice(
            positions, (zero_index, patch_slot, narrow_idx * rows_b), (3, 1, rows_b)
        )[:, 0]
        first_mod = select_rows(tables[0], kinds_a)
        entry_rows = (normalize(x_in) * (1.0 + first_mod[:, 1]) + first_mod[:, 0]).astype(
            jnp.bfloat16
        )
        qkv_terms = jnp.dot(
            lax.all_gather(entry_rows, "wide", axis=0, tiled=True),
            qkv_block,
            preferred_element_type=jnp.float32,
        )
        qkv = (
            lax.psum_scatter(
                qkv_terms.astype(jnp.bfloat16), "narrow", scatter_dimension=0, tiled=True
            )
            .astype(jnp.float32)
            .reshape(rows_b, heads_local, 3, head_dim)
        )
        angles = rotary_angles(positions_b, head_dim)
        queries = rotate(head_norm(qkv[:, :, 0], norms[0], norms[1]), angles).astype(jnp.bfloat16)
        fresh_keys = rotate(head_norm(qkv[:, :, 1], norms[2], norms[3]), angles).astype(
            jnp.bfloat16
        )
        fresh_values = qkv[:, :, 2].astype(jnp.bfloat16)
        fresh_pairs = jnp.concatenate([fresh_keys, fresh_values], axis=-1)
        cache_updated = lax.dynamic_update_slice(
            cache_now,
            fresh_pairs[None, None],
            (zero_index, patch_slot, zero_index, zero_index, zero_index),
        )
        local_pairs = cache_updated[0]
        query_req = kinds_b // 2
        start_carry = (
            jnp.full((rows_b, heads_local), NEG_FILL, jnp.float32),
            jnp.zeros((rows_b, heads_local), jnp.float32),
            jnp.zeros((rows_b, heads_local, head_dim), jnp.float32),
        )
        piece = lax.all_gather(local_pairs, "narrow", axis=1, tiled=True)
        count = piece.shape[1]
        key_req = (row_kind // 2).reshape(-1)
        keys_flat = piece.reshape(patch_count * count, heads_local, 2 * head_dim)
        top_all, total_all, accum_all = combine_parts(
            start_carry, partial_softmax(queries, query_req, keys_flat, key_req, head_dim)
        )
        attended = (
            (accum_all / total_all[..., None])
            .reshape(rows_b, heads_local * head_dim)
            .astype(jnp.bfloat16)
        )
        proj_terms = jnp.dot(
            lax.all_gather(attended, "narrow", axis=0, tiled=True),
            out_block,
            preferred_element_type=jnp.float32,
        )
        projected = lax.psum_scatter(
            proj_terms.astype(jnp.bfloat16), "wide", scatter_dimension=0, tiled=True
        ).astype(jnp.float32)
        after_attn = x_in + first_mod[:, 2] * projected
        second_mod = select_rows(tables[1], kinds_a)
        entry_second = (normalize(after_attn) * (1.0 + second_mod[:, 1]) + second_mod[:, 0]).astype(
            jnp.bfloat16
        )
        up_terms = jnp.dot(
            lax.all_gather(entry_second, "wide", axis=0, tiled=True),
            up_block,
            preferred_element_type=jnp.float32,
        )
        up_sum = lax.psum_scatter(
            up_terms.astype(jnp.bfloat16), "narrow", scatter_dimension=0, tiled=True
        ).astype(jnp.float32)
        hidden_act = jax.nn.gelu(up_sum, approximate=True).astype(jnp.bfloat16)
        down_terms = jnp.dot(
            lax.all_gather(hidden_act, "narrow", axis=0, tiled=True),
            down_block,
            preferred_element_type=jnp.float32,
        )
        down_sum = lax.psum_scatter(
            down_terms.astype(jnp.bfloat16), "wide", scatter_dimension=0, tiled=True
        ).astype(jnp.float32)
        layer_result = (after_attn + second_mod[:, 2] * down_sum).astype(jnp.bfloat16)
        written = lax.dynamic_update_slice(
            outputs, layer_result[None, None], (zero_index, patch_slot, zero_index, zero_index)
        )
        outputs = jnp.where(is_live, written, outputs)
        cache_now = jnp.where(is_live, cache_updated, cache_now)
        if step_index + 1 < step_total:
            arriving = passed_along(layer_result, "section", 1)
    return (outputs, cache_now)


def solution(mesh):
    in_specs = (
        P(None, "wide", "narrow"),
        P(),
        P(),
        P(),
        P("section", None, "narrow", "wide", None),
        P("section", "narrow", "wide"),
        P("section", None, None),
        P("section", "wide", "narrow"),
        P("section", None, None, None, "narrow"),
        P("section", "narrow", "wide"),
        P("section", "wide", "narrow"),
    )
    out_specs = (P("section", None, "wide", "narrow"), P("section", None, "narrow", "wide", None))
    return jax.shard_map(
        per_device, mesh=mesh, in_specs=in_specs, out_specs=out_specs, check_vma=False
    )
```

profile of v0, /device:TPU:17, one launch (start us, length us, event | category | flops | bytes accessed | tf_op | source)
XLA Modules:
  0.0 1330.5 jit_solution(3379327064187994064)
XLA Ops:
  32.3 19.3 %all_gather.45 = bf16[1024,384]{1,0:T(8,128)(2,1)S(1)} all-gather(bf16[64,384]{1,0:T(8,128)(2,1)S(1)} %fusion.104), channel_id=1, replica_groups=mesh['section'=2,'wide'=16,'narrow'=8] {'wide'}, dimensions={0}, use_global_device_ids=true | all-gather | bytes 835584 | tf_op jit(solution)/shard_map/all_gather | solution.py:148
  56.8 37.3 %reduce-scatter.37.cloned.1.call-done = bf16[128,576]{1,0:T(8,128)(2,1)} async-done(((bf16[1024,576]{1,0:T(8,128)(2,1)}), bf16[128,576]{1,0:T(8,128)(2,1)}) %reduce-scatter.37.cloned.1.call-update) | async-done | bytes 147472
  98.6 37.3 %all-gather.16.cloned.1.call-done = bf16[1,2,1024,3,128]{4,2,3,1,0:T(8,128)(2,1)} async-done(((bf16[1,2,128,3,128]{4,2,3,1,0:T(8,128)(2,1)}), bf16[1,2,1024,3,128]{4,2,3,1,0:T(8,128)(2,1)}) %all-gather.16.cloned.1.call-update) | async-done | bytes 1572880 | tf_op jit(solution)/shard_map/all_gather | solution.py:178
  164.8 83.2 %reduce-scatter.19.cloned.1.call-done = bf16[64,384]{1,0:T(8,128)(2,1)} async-done(((bf16[1024,384]{1,0:T(8,128)(2,1)}), bf16[64,384]{1,0:T(8,128)(2,1)}) %reduce-scatter.19.cloned.1.call-update) | async-done | bytes 49168 | tf_op jit(solution)/shard_map/reduce_scatter | solution.py:195
  262.9 18.1 %all_gather.48 = bf16[1024,384]{1,0:T(8,128)(2,1)S(1)} all-gather(bf16[64,384]{1,0:T(8,128)(2,1)S(1)} %fusion.135), channel_id=1, replica_groups=mesh['section'=2,'wide'=16,'narrow'=8] {'wide'}, dimensions={0}, use_global_device_ids=true | all-gather | bytes 835584 | tf_op jit(solution)/shard_map/all_gather | solution.py:204
  283.2 44.6 %reduce-scatter.21.cloned.1.call-done = bf16[128,768]{1,0:T(8,128)(2,1)} async-done(((bf16[1024,768]{1,0:T(8,128)(2,1)}), bf16[128,768]{1,0:T(8,128)(2,1)}) %reduce-scatter.21.cloned.1.call-update) | async-done | bytes 196624 | tf_op jit(solution)/shard_map/reduce_scatter | solution.py:208
  329.7 38.7 %all-gather.10.cloned.1.call-done = bf16[1024,768]{1,0:T(8,128)(2,1)} async-done(((bf16[128,768]{1,0:T(8,128)(2,1)}), bf16[1024,768]{1,0:T(8,128)(2,1)}) %all-gather.10.cloned.1.call-update) | async-done | bytes 1572880 | tf_op jit(solution)/shard_map/all_gather | solution.py:213
  371.8 77.6 %reduce-scatter.23.cloned.1.call-done = bf16[64,384]{1,0:T(8,128)(2,1)} async-done(((bf16[1024,384]{1,0:T(8,128)(2,1)}), bf16[64,384]{1,0:T(8,128)(2,1)}) %reduce-scatter.23.cloned.1.call-update) | async-done | bytes 49168 | tf_op jit(solution)/shard_map/reduce_scatter | solution.py:217
  469.2 17.8 %all_gather.50 = bf16[1024,384]{1,0:T(8,128)(2,1)S(1)} all-gather(bf16[64,384]{1,0:T(8,128)(2,1)S(1)} %fusion.109), channel_id=1, replica_groups=mesh['section'=2,'wide'=16,'narrow'=8] {'wide'}, dimensions={0}, use_global_device_ids=true | all-gather | bytes 835584 | tf_op jit(solution)/shard_map/all_gather | solution.py:148
  490.3 40.3 %reduce-scatter.39.cloned.1.call-done = bf16[128,576]{1,0:T(8,128)(2,1)} async-done(((bf16[1024,576]{1,0:T(8,128)(2,1)}), bf16[128,576]{1,0:T(8,128)(2,1)}) %reduce-scatter.39.cloned.1.call-update) | async-done | bytes 147472
  533.6 38.8 %all-gather.18.cloned.1.call-done = bf16[1,2,1024,3,128]{4,2,3,1,0:T(8,128)(2,1)} async-done(((bf16[1,2,128,3,128]{4,2,3,1,0:T(8,128)(2,1)}), bf16[1,2,1024,3,128]{4,2,3,1,0:T(8,128)(2,1)}) %all-gather.18.cloned.1.call-update) | async-done | bytes 1572880 | tf_op jit(solution)/shard_map/all_gather | solution.py:178
  601.5 83.2 %reduce-scatter.25.cloned.1.call-done = bf16[64,384]{1,0:T(8,128)(2,1)} async-done(((bf16[1024,384]{1,0:T(8,128)(2,1)}), bf16[64,384]{1,0:T(8,128)(2,1)}) %reduce-scatter.25.cloned.1.call-update) | async-done | bytes 49168 | tf_op jit(solution)/shard_map/reduce_scatter | solution.py:195
  699.5 18.1 %all_gather.53 = bf16[1024,384]{1,0:T(8,128)(2,1)S(1)} all-gather(bf16[64,384]{1,0:T(8,128)(2,1)S(1)} %fusion.126), channel_id=1, replica_groups=mesh['section'=2,'wide'=16,'narrow'=8] {'wide'}, dimensions={0}, use_global_device_ids=true | all-gather | bytes 835584 | tf_op jit(solution)/shard_map/all_gather | solution.py:204
  719.9 44.7 %reduce-scatter.27.cloned.1.call-done = bf16[128,768]{1,0:T(8,128)(2,1)} async-done(((bf16[1024,768]{1,0:T(8,128)(2,1)}), bf16[128,768]{1,0:T(8,128)(2,1)}) %reduce-scatter.27.cloned.1.call-update) | async-done | bytes 196624 | tf_op jit(solution)/shard_map/reduce_scatter | solution.py:208
  766.4 38.8 %all-gather.12.cloned.1.call-done = bf16[1024,768]{1,0:T(8,128)(2,1)} async-done(((bf16[128,768]{1,0:T(8,128)(2,1)}), bf16[1024,768]{1,0:T(8,128)(2,1)}) %all-gather.12.cloned.1.call-update) | async-done | bytes 1572880 | tf_op jit(solution)/shard_map/all_gather | solution.py:213
  808.5 77.6 %reduce-scatter.29.cloned.1.call-done = bf16[64,384]{1,0:T(8,128)(2,1)} async-done(((bf16[1024,384]{1,0:T(8,128)(2,1)}), bf16[64,384]{1,0:T(8,128)(2,1)}) %reduce-scatter.29.cloned.1.call-update) | async-done | bytes 49168 | tf_op jit(solution)/shard_map/reduce_scatter | solution.py:217
  905.8 17.7 %all_gather.55 = bf16[1024,384]{1,0:T(8,128)(2,1)S(1)} all-gather(bf16[64,384]{1,0:T(8,128)(2,1)S(1)} %fusion.114), channel_id=1, replica_groups=mesh['section'=2,'wide'=16,'narrow'=8] {'wide'}, dimensions={0}, use_global_device_ids=true | all-gather | bytes 835584 | tf_op jit(solution)/shard_map/all_gather | solution.py:148
  926.0 41.0 %reduce-scatter.41.cloned.1.call-done = bf16[128,576]{1,0:T(8,128)(2,1)} async-done(((bf16[1024,576]{1,0:T(8,128)(2,1)}), bf16[128,576]{1,0:T(8,128)(2,1)}) %reduce-scatter.41.cloned.1.call-update) | async-done | bytes 147472
  970.3 38.5 %all-gather.20.cloned.1.call-done = bf16[1,2,1024,3,128]{4,2,3,1,0:T(8,128)(2,1)} async-done(((bf16[1,2,128,3,128]{4,2,3,1,0:T(8,128)(2,1)}), bf16[1,2,1024,3,128]{4,2,3,1,0:T(8,128)(2,1)}) %all-gather.20.cloned.1.call-update) | async-done | bytes 1572880 | tf_op jit(solution)/shard_map/all_gather | solution.py:178
  1037.8 83.2 %reduce-scatter.31.cloned.1.call-done = bf16[64,384]{1,0:T(8,128)(2,1)} async-done(((bf16[1024,384]{1,0:T(8,128)(2,1)}), bf16[64,384]{1,0:T(8,128)(2,1)}) %reduce-scatter.31.cloned.1.call-update) | async-done | bytes 49168 | tf_op jit(solution)/shard_map/reduce_scatter | solution.py:195
  1135.7 18.1 %all_gather.58 = bf16[1024,384]{1,0:T(8,128)(2,1)S(1)} all-gather(bf16[64,384]{1,0:T(8,128)(2,1)S(1)} %fusion.117), channel_id=1, replica_groups=mesh['section'=2,'wide'=16,'narrow'=8] {'wide'}, dimensions={0}, use_global_device_ids=true | all-gather | bytes 835584 | tf_op jit(solution)/shard_map/all_gather | solution.py:204
  1156.1 44.6 %reduce-scatter.33.cloned.1.call-done = bf16[128,768]{1,0:T(8,128)(2,1)} async-done(((bf16[1024,768]{1,0:T(8,128)(2,1)}), bf16[128,768]{1,0:T(8,128)(2,1)}) %reduce-scatter.33.cloned.1.call-update) | async-done | bytes 196624 | tf_op jit(solution)/shard_map/reduce_scatter | solution.py:208
  1202.5 38.7 %all-gather.14.cloned.1.call-done = bf16[1024,768]{1,0:T(8,128)(2,1)} async-done(((bf16[128,768]{1,0:T(8,128)(2,1)}), bf16[1024,768]{1,0:T(8,128)(2,1)}) %all-gather.14.cloned.1.call-update) | async-done | bytes 1572880 | tf_op jit(solution)/shard_map/all_gather | solution.py:213
  1245.3 76.9 %reduce-scatter.35.cloned.1.call-done = bf16[64,384]{1,0:T(8,128)(2,1)} async-done(((bf16[1024,384]{1,0:T(8,128)(2,1)}), bf16[64,384]{1,0:T(8,128)(2,1)}) %reduce-scatter.35.cloned.1.call-update) | async-done | bytes 49168 | tf_op jit(solution)/shard_map/reduce_scatter | solution.py:217
  (302 shorter events, 240.7 us)
Async XLA Ops:
  7.2 273.9 %copy-start = (bf16[1,384,768]{2,1,0:T(8,128)(2,1)S(1)}, bf16[1,384,768]{2,1,0:T(8,128)(2,1)}, u32[]{:S(2)}) copy-start(bf16[1,384,768]{2,1,0:T(8,128)(2,1)} %param.20) | copy-start | bytes 1769476
  7.2 86.9 %reduce-scatter.37.cloned.1.call-start = ((), (), s32[]{:S(2)}) async-start(), calls=%async_computation.27 | async-start | bytes 1474560
  53.9 82.0 %all-gather.16.cloned.1.call-start = ((), (), s32[]{:S(2)}) async-start(), calls=%async_computation.24 | async-start | bytes 1769472 | tf_op jit(solution)/shard_map/all_gather | solution.py:178
  96.9 151.1 %reduce-scatter.19.cloned.1.call-start = ((), (), s32[]{:S(2)}) async-start(), calls=%async_computation.12 | async-start | bytes 835584 | tf_op jit(solution)/shard_map/reduce_scatter | solution.py:195
  164.8 163.1 %reduce-scatter.21.cloned.1.call-start = ((), (), s32[]{:S(2)}) async-start(), calls=%async_computation.13 | async-start | bytes 1769472 | tf_op jit(solution)/shard_map/reduce_scatter | solution.py:208
  283.2 85.2 %all-gather.10.cloned.1.call-start = ((), (), s32[]{:S(2)}) async-start(), calls=%async_computation.14 | async-start | bytes 1769472 | tf_op jit(solution)/shard_map/all_gather | solution.py:213
  329.6 139.5 %copy-start.14 = (f32[64,3,384]{2,0,1:T(8,128)S(1)}, f32[64,3,384]{2,0,1:T(8,128)}, u32[]{:S(2)}) copy-start(f32[64,3,384]{2,0,1:T(8,128)} %get-tuple-element.28) | copy-start | bytes 884740
  329.6 119.7 %reduce-scatter.23.cloned.1.call-start = ((), (), s32[]{:S(2)}) async-start(), calls=%async_computation.15 | async-start | bytes 835584 | tf_op jit(solution)/shard_map/reduce_scatter | solution.py:217
  371.7 158.8 %reduce-scatter.39.cloned.1.call-start = ((), (), s32[]{:S(2)}) async-start(), calls=%async_computation.28 | async-start | bytes 1474560
  450.2 4.9 collective-permute-start
  489.4 83.0 %all-gather.18.cloned.1.call-start = ((), (), s32[]{:S(2)}) async-start(), calls=%async_computation.25 | async-start | bytes 1769472 | tf_op jit(solution)/shard_map/all_gather | solution.py:178
  533.4 151.3 %reduce-scatter.25.cloned.1.call-start = ((), (), s32[]{:S(2)}) async-start(), calls=%async_computation.16 | async-start | bytes 835584 | tf_op jit(solution)/shard_map/reduce_scatter | solution.py:195
  601.4 163.1 %reduce-scatter.27.cloned.1.call-start = ((), (), s32[]{:S(2)}) async-start(), calls=%async_computation.17 | async-start | bytes 1769472 | tf_op jit(solution)/shard_map/reduce_scatter | solution.py:208
  719.8 85.3 %all-gather.12.cloned.1.call-start = ((), (), s32[]{:S(2)}) async-start(), calls=%async_computation.18 | async-start | bytes 1769472 | tf_op jit(solution)/shard_map/all_gather | solution.py:213
  766.3 119.8 %copy-start.27 = (bf16[1,2,64,384]{3,2,1,0:T(8,128)(2,1)S(1)}, bf16[1,2,64,384]{3,2,1,0:T(8,128)(2,1)}, u32[]{:S(2)}) copy-start(bf16[1,2,64,384]{3,2,1,0:T(8,128)(2,1)} %copy-done.26) | copy-start | bytes 294916
  766.3 119.8 %reduce-scatter.29.cloned.1.call-start = ((), (), s32[]{:S(2)}) async-start(), calls=%async_computation.19 | async-start | bytes 835584 | tf_op jit(solution)/shard_map/reduce_scatter | solution.py:217
  808.4 158.6 %reduce-scatter.41.cloned.1.call-start = ((), (), s32[]{:S(2)}) async-start(), calls=%async_computation.29 | async-start | bytes 1474560
  886.9 4.9 collective-permute-start.1
  925.8 83.0 %all-gather.20.cloned.1.call-start = ((), (), s32[]{:S(2)}) async-start(), calls=%async_computation.26 | async-start | bytes 1769472 | tf_op jit(solution)/shard_map/all_gather | solution.py:178
  969.9 151.1 %reduce-scatter.31.cloned.1.call-start = ((), (), s32[]{:S(2)}) async-start(), calls=%async_computation.20 | async-start | bytes 835584 | tf_op jit(solution)/shard_map/reduce_scatter | solution.py:195
  1037.7 162.9 %reduce-scatter.33.cloned.1.call-start = ((), (), s32[]{:S(2)}) async-start(), calls=%async_computation.21 | async-start | bytes 1769472 | tf_op jit(solution)/shard_map/reduce_scatter | solution.py:208
  1156.0 85.2 %all-gather.14.cloned.1.call-start = ((), (), s32[]{:S(2)}) async-start(), calls=%async_computation.22 | async-start | bytes 1769472 | tf_op jit(solution)/shard_map/all_gather | solution.py:213
  1202.5 119.7 %copy-start.29 = (bf16[1,2,64,384]{3,2,1,0:T(8,128)(2,1)S(1)}, bf16[1,2,64,384]{3,2,1,0:T(8,128)(2,1)}, u32[]{:S(2)}) copy-start(bf16[1,2,64,384]{3,2,1,0:T(8,128)(2,1)} %copy-done.28) | copy-start | bytes 294916
  1202.5 119.7 %reduce-scatter.35.cloned.1.call-start = ((), (), s32[]{:S(2)}) async-start(), calls=%async_computation.23 | async-start | bytes 835584 | tf_op jit(solution)/shard_map/reduce_scatter | solution.py:217
  (49 other events, 1646.2 us)
Sparse Core Ops, SparseCore 0:
  54.0 40.0 reduce-scatter.36
  97.1 38.7 all-gather.15
  164.9 83.0 reduce-scatter.18
  283.3 44.5 reduce-scatter.20
  329.7 38.6 all-gather.9
  371.8 77.4 reduce-scatter.22
  489.5 41.0 reduce-scatter.38
  533.5 38.8 all-gather.17
  601.5 83.1 reduce-scatter.24
  719.9 44.5 reduce-scatter.26
  766.4 38.6 all-gather.11
  808.5 77.4 reduce-scatter.28
  925.9 41.0 reduce-scatter.40
  970.0 38.7 all-gather.19
  1037.9 83.1 reduce-scatter.30
  1156.1 44.5 reduce-scatter.32
  1202.6 38.6 all-gather.13
  1244.7 77.4 reduce-scatter.34
where the time goes:
time: 1330 us
  waiting for transfers between devices  973 us (73%)
  blocking collectives  246 us (18%)
  matrix products  34.3 us (3%)
  local copies, waits for them, and re-layouts  33.2 us (2%)
  other arithmetic  25.7 us (2%)
  between operations  15.6 us (1%)
    reduce_scatter x3, waiting for transfers between devices, per_device(): lax.psum_scatter(proj_terms.astype(jnp.bfloat16), 'wide', scatter_dimensi...  250 us
    reduce_scatter x3, waiting for transfers between devices, per_device(): lax.psum_scatter(down_terms.astype(jnp.bfloat16), 'wide', scatter_dimensi...  232 us
    reduce_scatter x3, waiting for transfers between devices, per_device(): lax.psum_scatter(up_terms.astype(jnp.bfloat16), 'narrow', scatter_dimensi...  134 us
    unnamed x21, waiting for transfers between devices  119 us
    all_gather x3, waiting for transfers between devices, per_device(): lax.all_gather(hidden_act, 'narrow', axis=0, tiled=True)  116 us
    all_gather x3, waiting for transfers between devices, per_device(): piece = lax.all_gather(local_pairs, 'narrow', axis=1, tiled=True)  115 us
    psum x6, blocking collectives, normalize(): lax.psum((jnp.sum(values, axis=1), jnp.sum(values * values, axis=1)), 'na...  85.3 us
    all_gather x3, blocking collectives, per_device(): lax.all_gather(entry_rows, 'wide', axis=0, tiled=True)  54.7 us
  transfers between devices with their start and end apart: 20, of which 20 were waited for; matrix products, arithmetic and copies ran while one was open for 0% of the time, Pallas kernels for 0%

commit v1 on v0

v1 whole, which is shorter than its diff:
```python
import functools

import jax
import jax.numpy as jnp
from jax import lax
from jax.experimental import pallas as pl
from jax.experimental.pallas import tpu as pltpu
from jax.sharding import PartitionSpec as P

EPS_ROW = 1e-05
EPS_HEAD = 1e-06
NEG_FILL = -1e30
F32 = jnp.float32
BF16 = jnp.bfloat16


def time_features(timesteps, feature_count):
    half_count = feature_count // 2
    frequency = jnp.exp(-jnp.log(10000.0) * jnp.arange(half_count, dtype=F32) / half_count)
    angle = timesteps.astype(F32)[:, None] * frequency[None, :]
    return jnp.concatenate([jnp.cos(angle), jnp.sin(angle)], axis=1)


def rotary_angles(row_positions, head_dim):
    dim_frame = head_dim // 4
    dim_plane = head_dim // 8 * 3
    pieces = []
    for axis_pos, span_dims in ((0, dim_frame), (1, dim_plane), (2, dim_plane)):
        frequency = 10000.0 ** (-jnp.arange(0, span_dims, 2, dtype=F32) / span_dims)
        pieces.append(row_positions[axis_pos].astype(F32)[:, None] * frequency[None, :])
    return jnp.concatenate(pieces, axis=1)


def two_layers(
    nw,
    nn,
    hid,
    tab_in,
    rope,
    kinda,
    qreq,
    kreq,
    stale,
    wq_in,
    wo_in,
    wu_in,
    wd_in,
    lo_ref,
    nc_ref,
    tab,
    wq,
    wo,
    wu,
    wd,
    stat_own,
    stat_all,
    entry,
    kv,
    att,
    act,
    part_out,
    part_in,
    rs_send_q,
    rs_recv_q,
    rs_send_u,
    rs_recv_u,
    x_now,
    w_sem,
    w_send,
    stat_sem,
    agw_sem,
    rsw_sem,
    rsz_send,
    rsz_recv,
    agz_send,
    agz_recv,
    stale_sem,
    stale_send,
    sis_sem,
    sis_send,
    out_sem,
    out_send,
):
    sec = lax.axis_index("section")
    w = lax.axis_index("wide")
    n = lax.axis_index("narrow")
    rows_a, feat = x_now.shape
    rows_b = rope.shape[1]
    per_block = rows_b // rows_a
    heads = kv.shape[-1] // 128
    width = feat * nn
    half = nn // 2
    other = 1 - sec
    right = lax.rem(n + 1, nn)
    left = lax.rem(n + nn - 1, nn)

    def blk(offset):
        return lax.rem(n + offset + 2 * nn, nn)

    def remote(src, dst, send_sem, recv_sem, where):
        return pltpu.make_async_remote_copy(
            src_ref=src,
            dst_ref=dst,
            send_sem=send_sem,
            recv_sem=recv_sem,
            device_id=where,
            device_id_type=pl.DeviceIdType.MESH,
        )

    def drain(ref, sem):
        pltpu.make_async_copy(ref, ref, sem).wait()

    barrier = pltpu.get_barrier_semaphore()
    for j in range(1, nw):
        pl.semaphore_signal(barrier, inc=1, device_id={"wide": lax.rem(w + j, nw)})
    for j in range(1, nn):
        pl.semaphore_signal(barrier, inc=1, device_id={"narrow": blk(j)})
    for j in range(nn):
        pl.semaphore_signal(barrier, inc=1, device_id={"section": other, "narrow": blk(j)})
    pl.semaphore_wait(barrier, nw - 1 + nn - 1 + nn)

    pairs = ((tab_in, tab), (wq_in, wq), (wo_in, wo), (wu_in, wu), (wd_in, wd))
    for i, (source, held) in enumerate(pairs):
        pltpu.make_async_copy(source, held.at[sec], w_sem.at[i, sec]).start()
        remote(
            source, held.at[sec], w_send.at[i], w_sem.at[i, sec], {"section": other}
        ).start()

    lanes = lax.broadcasted_iota(jnp.int32, (rows_b, 128), 1)
    low = lanes < 64
    even = lax.rem(lanes, 2) == 0
    kind_col = kinda[...]

    def row_table(l, norm_index, j):
        base = norm_index * 12 + j
        out = jnp.zeros((rows_a, feat), F32)
        for kind in range(4):
            value = tab[l, base + 3 * kind : base + 3 * kind + 1, :]
            out = jnp.where(kind_col == kind, value, out)
        return out

    def normalize(l, norm_index, x):
        total = jnp.sum(x, axis=1, keepdims=True)
        square = jnp.sum(x * x, axis=1, keepdims=True)
        place = lax.broadcasted_iota(jnp.int32, (rows_a, 128), 1)
        packed = jnp.where(place == 0, total, jnp.where(place == 1, square, 0.0))
        packed = jnp.concatenate([packed, jnp.zeros((128 - rows_a, 128), F32)], axis=0)
        turned = packed.T[0:8, :]
        stat_own[l, norm_index] = turned
        for j in range(1, nn):
            remote(
                stat_own.at[l, norm_index],
                stat_all.at[l, norm_index, n],
                stat_sem.at[l, norm_index, 0],
                stat_sem.at[l, norm_index, 1],
                {"narrow": blk(j)},
            ).start()
        stat_all[l, norm_index, n] = turned
        drain(stat_all.at[l, norm_index, pl.ds(0, nn - 1)], stat_sem.at[l, norm_index, 1])
        summed = stat_all[l, norm_index, 0]
        for j in range(1, nn):
            summed = summed + stat_all[l, norm_index, j]
        drain(stat_all.at[l, norm_index, pl.ds(0, nn - 1)], stat_sem.at[l, norm_index, 0])
        back = jnp.concatenate([summed, jnp.zeros((120, 128), F32)], axis=0).T
        row_mean = back[0:rows_a, 0:1] / width
        variance = back[0:rows_a, 1:2] / width - row_mean * row_mean
        return (x - row_mean) * lax.rsqrt(variance + EPS_ROW)

    def gather_wide(l, norm_index, x):
        scale = row_table(l, norm_index, 1)
        shift = row_table(l, norm_index, 0)
        normed = normalize(l, norm_index, x)
        entry[l, norm_index, w] = (normed * (1.0 + scale) + shift).astype(BF16)
        for j in range(1, nw):
            remote(
                entry.at[l, norm_index, w],
                entry.at[l, norm_index, w],
                agw_sem.at[l, norm_index, 0],
                agw_sem.at[l, norm_index, 1],
                {"wide": lax.rem(w + j, nw)},
            ).start()

    def gather_wide_done(l, norm_index):
        many = entry.at[l, norm_index, pl.ds(0, nw - 1)]
        drain(many, agw_sem.at[l, norm_index, 1])
        drain(many, agw_sem.at[l, norm_index, 0])

    def scatter_narrow(l, norm_index, weight, send, recv):
        def term(m):
            rows = entry[l, norm_index, pl.ds(m * per_block, per_block)].reshape(rows_b, feat)
            return jnp.dot(rows, weight[l], preferred_element_type=F32)

        def hop(side, k):
            return remote(
                send.at[side, k],
                recv.at[side, k],
                rsz_send.at[l, norm_index, side, k],
                rsz_recv.at[l, norm_index, side, k],
                {"narrow": right if side == 0 else left},
            )

        for k in range(half):
            for side in range(2):
                steps = half if side == 0 else half - 1
                if k >= steps:
                    continue
                target = blk(half - k) if side == 0 else blk(k - (half - 1))
                value = term(target)
                if k > 0:
                    hop(side, k - 1).wait_recv()
                    value = value + recv[side, k - 1].astype(F32)
                if True:
                    send[side, k] = value.astype(BF16)
                hop(side, k).start()
        total = term(n)
        for side in range(2):
            steps = half if side == 0 else half - 1
            if steps > 0:
                hop(side, steps - 1).wait_recv()
                total = total + recv[side, steps - 1].astype(F32)
        for side in range(2):
            steps = half if side == 0 else half - 1
            for k in range(steps):
                hop(side, k).wait_send()
        return total

    def gather_narrow(l, which, buffer, on_block):
        def hop(side, k, block):
            return remote(
                buffer.at[block],
                buffer.at[block],
                agz_send.at[l, which, side, k],
                agz_recv.at[l, which, side, k],
                {"narrow": right if side == 0 else left},
            )

        hop(0, 0, n).start()
        if half > 1:
            hop(1, 0, n).start()
        on_block(n)
        for k in range(half):
            from_left = blk(-1 - k)
            hop(0, k, from_left).wait_recv()
            if k + 1 < half:
                hop(0, k + 1, from_left).start()
            if k + 1 < half:
                from_right = blk(1 + k)
                hop(1, k, from_right).wait_recv()
                if k + 2 < half:
                    hop(1, k + 1, from_right).start()
            on_block(from_left)
            if k + 1 < half:
                on_block(from_right)
        for k in range(half):
            hop(0, k, n).wait_send()
            if k + 1 < half:
                hop(1, k, n).wait_send()

    def scatter_wide(l, which, weight, values):
        def on_block(m):
            terms = jnp.dot(values[m], weight[l], preferred_element_type=F32).astype(BF16)
            for i in range(per_block):
                target = m * per_block + i
                piece = terms[i * rows_a : (i + 1) * rows_a]

                @pl.when(target == w)
                def _():
                    part_in[l, which, w] = piece

                @pl.when(target != w)
                def _():
                    part_out[l, which, target] = piece
                    remote(
                        part_out.at[l, which, target],
                        part_in.at[l, which, w],
                        rsw_sem.at[l, which, 0],
                        rsw_sem.at[l, which, 1],
                        {"wide": target},
                    ).start()

        return on_block

    def scatter_wide_done(l, which):
        many = part_in.at[l, which, pl.ds(0, nw - 1)]
        drain(many, rsw_sem.at[l, which, 1])
        total = part_in[l, which, 0].astype(F32)
        for j in range(1, nw):
            total = total + part_in[l, which, j].astype(F32)
        drain(many, rsw_sem.at[l, which, 0])
        return total

    def send_stale(l):
        @pl.when(sec == l)
        def _():
            for j in range(nn):
                if l == 0 and j == 0:
                    pltpu.make_async_copy(
                        stale.at[1], kv.at[l, 1, n], stale_sem.at[l]
                    ).start()
                else:
                    remote(
                        stale.at[1],
                        kv.at[l, 1, n],
                        stale_send.at[l],
                        stale_sem.at[l],
                        {"section": 0, "narrow": blk(j)},
                    ).start()

    def send_result(l, kind, source, target):
        @pl.when(sec == l)
        def _():
            pltpu.make_async_copy(source, target.at[sec], out_sem.at[l, kind, sec]).start()

        @pl.when(sec != l)
        def _():
            remote(
                source,
                target.at[sec],
                out_send.at[l, kind],
                out_sem.at[l, kind, sec],
                {"section": other},
            ).start()

    for l in range(2):
        if l == 0:
            x_in = hid[sec].astype(F32)
            drain(tab.at[0], w_sem.at[0, 0])
            drain(tab.at[1], w_sem.at[0, 1])
        else:
            x_in = x_now[...].astype(F32)
        gather_wide(l, 0, x_in)
        if l == 0:
            send_stale(0)
        first_gate = row_table(l, 0, 2)
        drain(wq.at[l], w_sem.at[1, l])
        gather_wide_done(l, 0)
        qkv = scatter_narrow(l, 0, wq, rs_send_q.at[l], rs_recv_q.at[l])
        gains = (tab[l, 24:25, 0:128], tab[l, 25:26, 0:128])
        cosine = rope[0]
        sine = rope[1]
        queries = []
        for h in range(heads):
            both = qkv[:, h * 192 : h * 192 + 128]
            upper = qkv[:, h * 192 + 64 : h * 192 + 192]

            def half_mean(values):
                first = jnp.sum(jnp.where(low, values, 0.0), axis=1, keepdims=True)
                second = jnp.sum(jnp.where(low, 0.0, values), axis=1, keepdims=True)
                return jnp.where(low, first, second) * (1.0 / 64)

            center = both - half_mean(both)
            spread = half_mean(center * center)
            normed = center * lax.rsqrt(spread + EPS_HEAD) * gains[0] + gains[1]
            swapped = jnp.where(
                even, pltpu.roll(normed, 127, 1), pltpu.roll(normed, 1, 1)
            )
            turned = normed * cosine + swapped * sine
            queries.append(jnp.where(low, turned * 0.125, 0.0).astype(BF16))
            kv[l, sec, n, :, h * 128 : (h + 1) * 128] = jnp.where(
                low, pltpu.roll(turned, 64, 1), upper
            ).astype(BF16)
        send_result(l, 0, kv.at[l, sec, n], nc_ref)

        def to_sister(m):
            @pl.when(sec == 0)
            def _():
                remote(
                    kv.at[l, 0, m],
                    kv.at[l, 0, m],
                    sis_send.at[l],
                    sis_sem.at[l],
                    {"section": 1},
                ).start()

        gather_narrow(l, 0, kv.at[l, sec], to_sister)
        if l == 0:
            send_stale(1)

        @pl.when(sec == 0)
        def _():
            drain(kv.at[l, 1], stale_sem.at[l])

        @pl.when(sec == 1)
        def _():
            drain(kv.at[l, 0], sis_sem.at[l])

        request = qreq[...]
        for h in range(heads):
            tops = []
            scores = []
            for p in range(2):
                pairs_h = kv[l, p, :, :, h * 128 : (h + 1) * 128].reshape(nn * rows_b, 128)
                raw = lax.dot_general(
                    queries[h], pairs_h, (((1,), (1,)), ((), ())), preferred_element_type=F32
                )
                raw = jnp.where(request == kreq[p : p + 1, :], raw, NEG_FILL)
                scores.append(raw)
                tops.append(jnp.max(raw, axis=1, keepdims=True))
            top = jnp.maximum(tops[0], tops[1])
            total = jnp.zeros((rows_b, 1), F32)
            mixed = jnp.zeros((rows_b, 128), F32)
            for p in range(2):
                pairs_h = kv[l, p, :, :, h * 128 : (h + 1) * 128].reshape(nn * rows_b, 128)
                weights = jnp.exp(scores[p] - top)
                total = total + jnp.sum(weights, axis=1, keepdims=True)
                mixed = mixed + jnp.dot(
                    weights.astype(BF16), pairs_h, preferred_element_type=F32
                )
            att[l, n, :, h * 64 : (h + 1) * 64] = (mixed / total)[:, 64:128].astype(BF16)
        drain(wo.at[l], w_sem.at[2, l])
        gather_narrow(l, 1, att.at[l], scatter_wide(l, 0, wo, att.at[l]))
        after = x_in + first_gate * scatter_wide_done(l, 0)
        gather_wide(l, 1, after)
        second_gate = row_table(l, 1, 2)
        drain(wu.at[l], w_sem.at[3, l])
        gather_wide_done(l, 1)
        up = scatter_narrow(l, 1, wu, rs_send_u.at[l], rs_recv_u.at[l])
        act[l, n] = jax.nn.gelu(up, approximate=True).astype(BF16)
        drain(wd.at[l], w_sem.at[4, l])
        gather_narrow(l, 2, act.at[l], scatter_wide(l, 1, wd, act.at[l]))
        result = (after + second_gate * scatter_wide_done(l, 1)).astype(BF16)
        if l == 0:
            x_now[...] = result
            send_result(l, 1, x_now, lo_ref)
        else:
            part_out[0, 0, w] = result
            send_result(l, 1, part_out.at[0, 0, w], lo_ref)

    for i, (source, held) in enumerate(pairs):
        drain(held.at[0], w_send.at[i])
    for l in range(2):

        @pl.when(sec == l)
        def _():
            drain(kv.at[l, 1, pl.ds(0, nn - 1 + l)], stale_send.at[l])
            for kind, target in ((0, nc_ref), (1, lo_ref)):
                for p in range(2):
                    drain(target.at[p], out_sem.at[l, kind, p])

        @pl.when(sec != l)
        def _():
            for kind, target in ((0, nc_ref), (1, lo_ref)):
                drain(target.at[0], out_send.at[l, kind])

        @pl.when(sec == 0)
        def _():
            drain(kv.at[l, 0], sis_send.at[l])


def per_device(
    hidden_in,
    row_kind,
    positions,
    timesteps,
    stale_cache,
    w_qkv,
    qk_norm,
    w_out,
    ada_weight,
    w_up,
    w_down,
):
    nw = lax.axis_size("wide")
    nn = lax.axis_size("narrow")
    w = lax.axis_index("wide")
    n = lax.axis_index("narrow")
    sec = lax.axis_index("section")
    _, rows_a, feat = hidden_in.shape
    rows_b = rows_a * nw // nn
    heads = stale_cache.shape[3]
    head_dim = stale_cache.shape[4] // 2
    pair_cols = heads * 2 * head_dim
    zero = jnp.zeros((), jnp.int32)
    activated = jax.nn.silu(time_features(timesteps, ada_weight.shape[2])).astype(BF16)
    modulation = jnp.einsum(
        "re,kesd->krsd", activated, ada_weight[0], preferred_element_type=F32
    )
    gains = jnp.concatenate(
        [
            jnp.concatenate([qk_norm[0, 0:1], qk_norm[0, 2:3]], axis=1),
            jnp.concatenate([qk_norm[0, 1:2], qk_norm[0, 3:4]], axis=1),
        ],
        axis=0,
    )
    tab_in = jnp.concatenate(
        [
            modulation.reshape(24, feat),
            jnp.pad(gains, ((0, 6), (0, feat - 2 * head_dim))),
        ],
        axis=0,
    )
    kinda = lax.dynamic_slice(row_kind, (sec, w * rows_a), (1, rows_a)).reshape(rows_a, 1)
    qreq = lax.dynamic_slice(row_kind, (sec, n * rows_b), (1, rows_b)).reshape(rows_b, 1) // 2
    kreq = row_kind // 2
    own_pos = lax.dynamic_slice(positions, (zero, sec, n * rows_b), (3, 1, rows_b))[:, 0]
    angles = rotary_angles(own_pos, head_dim)
    cosine = jnp.repeat(jnp.cos(angles), 2, axis=1)
    sine = jnp.repeat(jnp.sin(angles), 2, axis=1)
    sign = jnp.where(jnp.arange(head_dim) % 2 == 0, -1.0, 1.0).astype(F32)
    sine = sine * sign[None, :]
    rope = jnp.stack([jnp.tile(cosine, (1, 2)), jnp.tile(sine, (1, 2))], axis=0)
    stale = stale_cache.reshape(2, rows_b, pair_cols)
    cols_q = w_qkv.shape[2]
    cols_u = w_up.shape[2]
    cols_o = w_out.shape[1]
    half = nn // 2
    vm = pl.BlockSpec(memory_space=pltpu.VMEM)
    anywhere = pl.BlockSpec(memory_space=pl.ANY)
    dma = pltpu.SemaphoreType.DMA
    layer_out, cache_out = pl.pallas_call(
        functools.partial(two_layers, nw, nn),
        out_shape=(
            jax.ShapeDtypeStruct((2, rows_a, feat), BF16),
            jax.ShapeDtypeStruct((2, rows_b, pair_cols), BF16),
        ),
        in_specs=[vm, anywhere, vm, vm, vm, vm] + [anywhere] * 5,
        out_specs=(anywhere, anywhere),
        scratch_shapes=[
            pltpu.VMEM((2, 32, feat), F32),
            pltpu.VMEM((2, feat, cols_q), BF16),
            pltpu.VMEM((2, cols_o, feat), BF16),
            pltpu.VMEM((2, feat, cols_u), BF16),
            pltpu.VMEM((2, cols_u, feat), BF16),
            pltpu.VMEM((2, 2, 8, 128), F32),
            pltpu.VMEM((2, 2, nn, 8, 128), F32),
            pltpu.VMEM((2, 2, nw, rows_a, feat), BF16),
            pltpu.VMEM((2, 2, nn, rows_b, pair_cols), BF16),
            pltpu.VMEM((2, nn, rows_b, cols_o), BF16),
            pltpu.VMEM((2, nn, rows_b, cols_u), BF16),
            pltpu.VMEM((2, 2, nw, rows_a, feat), BF16),
            pltpu.VMEM((2, 2, nw, rows_a, feat), BF16),
            pltpu.VMEM((2, 2, half, rows_b, cols_q), BF16),
            pltpu.VMEM((2, 2, half, rows_b, cols_q), BF16),
            pltpu.VMEM((2, 2, half, rows_b, cols_u), BF16),
            pltpu.VMEM((2, 2, half, rows_b, cols_u), BF16),
            pltpu.VMEM((rows_a, feat), BF16),
            dma((5, 2)),
            dma((5,)),
            dma((2, 2, 2)),
            dma((2, 2, 2)),
            dma((2, 2, 2)),
            dma((2, 2, 2, half)),
            dma((2, 2, 2, half)),
            dma((2, 3, 2, half)),
            dma((2, 3, 2, half)),
            dma((2,)),
            dma((2,)),
            dma((2,)),
            dma((2,)),
            dma((2, 2, 2)),
            dma((2, 2)),
        ],
        compiler_params=pltpu.CompilerParams(
            collective_id=0, has_side_effects=True, vmem_limit_bytes=60 * 1024 * 1024
        ),
    )(
        hidden_in,
        tab_in,
        rope,
        kinda,
        qreq,
        kreq,
        stale,
        w_qkv[0],
        w_out[0],
        w_up[0],
        w_down[0],
    )
    return (
        layer_out[None],
        cache_out.reshape(1, 2, rows_b, heads, 2 * head_dim),
    )


def solution(mesh):
    in_specs = (
        P(None, "wide", "narrow"),
        P(),
        P(),
        P(),
        P("section", None, "narrow", "wide", None),
        P("section", "narrow", "wide"),
        P("section", None, None),
        P("section", "wide", "narrow"),
        P("section", None, None, None, "narrow"),
        P("section", "narrow", "wide"),
        P("section", "wide", "narrow"),
    )
    out_specs = (P("section", None, "wide", "narrow"), P("section", None, "narrow", "wide", None))
    return jax.shard_map(
        per_device, mesh=mesh, in_specs=in_specs, out_specs=out_specs, check_vma=False
    )
```

time: 1330 us -> 336 us (0.25)
  waiting for transfers between devices: 973 us -> 0 us
  Pallas kernels: 0 us -> 318 us
  blocking collectives: 246 us -> 0 us
  matrix products: 34.3 us -> 3.04 us
  local copies, waits for them, and re-layouts: 33.2 us -> 8.97 us
  other arithmetic: 25.7 us -> 5.24 us
  between operations: 15.6 us -> 0.75 us
    reduce_scatter x9 -> x0, waiting for transfers between devices: 616 us -> none  [the longest x3 250 us: per_device(): lax.psum_scatter(proj_terms.astype(jnp.bfloat16), 'wide', scatter_dimensi...]
    pallas_call x0 -> x1, Pallas kernels: none -> 318 us  [per_device(): pl.pallas_call(functools.partial(two_layers, nw, nn), out_shape=(jax.Shap...]
    all_gather x6 -> x0, waiting for transfers between devices: 231 us -> none  [the longest x3 116 us: per_device(): lax.all_gather(hidden_act, 'narrow', axis=0, tiled=True)]
    all_gather x9 -> x0, blocking collectives: 160 us -> none  [the longest x3 54.7 us: per_device(): lax.all_gather(entry_rows, 'wide', axis=0, tiled=True)]
    unnamed x21 -> x0, waiting for transfers between devices: 119 us -> none
    psum x6 -> x0, blocking collectives: 85.3 us -> none  [normalize(): lax.psum((jnp.sum(values, axis=1), jnp.sum(values * values, axis=1)), 'na...]
    dot_general x18 -> x0, matrix products: 31.2 us -> none  [the longest x3 9.82 us: per_device(): jnp.dot(lax.all_gather(hidden_act, 'narrow', axis=0, tiled=True), down_bl...]
  transfers between devices with their start and end apart: 20 -> 0, of which waited for: 20 -> 0; matrix products, arithmetic and copies ran while one was open for 0% -> 0% of each run, Pallas kernels for 0% -> 0%
where the time goes in v1:
time: 336 us
  Pallas kernels  318 us (95%)
  local copies, waits for them, and re-layouts  8.97 us (3%)
  other arithmetic  5.24 us (2%)
    pallas_call x1, Pallas kernels, per_device(): pl.pallas_call(functools.partial(two_layers, nw, nn), out_shape=(jax.Shap...  318 us

profile of v1, /device:TPU:17, one launch (start us, length us, event | category | flops | bytes accessed | tf_op | source)
XLA Modules:
  0.0 335.6 jit_solution(13351889434195974438)
XLA Ops:
  0.7 0.8 dynamic-slice_bitcast_fusion.1
  1.5 0.7 convert_element_type.38
  2.2 0.8 dynamic-slice_bitcast_fusion
  2.9 0.8 fusion.15
  3.8 0.8 slice_bitcast_fusion.3
  4.6 0.1 multiply_cosine_fusion
  4.8 1.3 and_select_fusion.kreq
  6.1 0.1 fusion.7
  6.2 0.1 fusion.9
  6.3 0.7 copy.31.kinda
  7.1 0.1 copy.23
  7.3 0.1 copy.24
  7.4 0.7 pad_maximum_fusion.rope
  8.0 3.0 fusion.2
  11.1 0.6 pad_maximum_fusion.1.tab_in
  11.7 0.1 copy.25
  11.9 0.7 add_select_fusion.qreq
  12.5 0.2 copy.29
  12.7 0.8 copy.32.stale
  13.5 1.0 copy.30
  14.5 317.6 %shard_map.122 = (bf16[2,64,384]{2,1,0:T(8,128)(2,1)}, bf16[2,128,384]{2,1,0:T(8,128)(2,1)}) custom-call(bf16[2,64,384]{2,1,0:T(8,128)(2,1)} %hid.1, f32[32,384]{1,0:T(8,128)} %pad_maximum_fusion.1.tab_in, f32[2,128,128]{2,1,0:T(8,128)} %pad_maximum_fusion.rope, s32[64,1]{1,0:T(8,128)} %copy.31.kinda, s32[128,1]{1,0:T(8,128)} %add_select_fusion.qreq, ...), custom_call_target="tpu_custom_call" | custom-call | tf_op jit(solution)/shard_map/pallas_call | solution.py:510
  332.1 1.1 copy.33
  333.2 0.8 copy.34
  334.0 1.5 copy.37
  (17 shorter events, 0.3 us)
Async XLA Ops:
  0.6 12.9 %copy-start = (bf16[1,384,576]{1,2,0:T(8,128)(2,1)S(1)}, bf16[1,384,576]{1,2,0:T(8,128)(2,1)}, u32[]{:S(2)}) copy-start(bf16[1,384,576]{1,2,0:T(8,128)(2,1)} %param.16) | copy-start | bytes 1327108
  0.6 11.9 %copy-start.1 = (bf16[1,2,128,3,128]{4,2,3,1,0:T(8,128)(2,1)S(1)}, bf16[1,2,128,3,128]{4,2,3,1,0:T(8,128)(2,1)}, u32[]{:S(2)}) copy-start(bf16[1,2,128,3,128]{4,2,3,1,0:T(8,128)(2,1)} %param.15) | copy-start | bytes 589828

commit v2 on v1

--- a/solution.py
+++ b/solution.py
@@ -185,76 +185,87 @@
         drain(many, agw_sem.at[l, norm_index, 1])
         drain(many, agw_sem.at[l, norm_index, 0])
 
-    def scatter_narrow(l, norm_index, weight, send, recv):
+    def rows_of(c):
+        return pl.ds(c * rows_a, rows_a)
+
+    def scatter_narrow(l, norm_index, weight, send, recv, on_half):
         def term(m):
             rows = entry[l, norm_index, pl.ds(m * per_block, per_block)].reshape(rows_b, feat)
             return jnp.dot(rows, weight[l], preferred_element_type=F32)
 
-        def hop(side, k):
+        def hop(side, k, c):
             return remote(
-                send.at[side, k],
-                recv.at[side, k],
-                rsz_send.at[l, norm_index, side, k],
-                rsz_recv.at[l, norm_index, side, k],
+                send.at[side, k, rows_of(c)],
+                recv.at[side, k, rows_of(c)],
+                rsz_send.at[l, norm_index, side, k, c],
+                rsz_recv.at[l, norm_index, side, k, c],
                 {"narrow": right if side == 0 else left},
             )
 
         for k in range(half):
+            if k == 0:
+                shared = term(blk(half))
+                values = (shared, shared)
+            else:
+                values = (term(blk(half - k)), term(blk(k - half)))
+            for stage in range(2):
+                for side in range(2):
+                    c = 1 - side if stage == 0 else side
+                    if k == 0 and c != side:
+                        continue
+                    value = values[side][c * rows_a : (c + 1) * rows_a]
+                    if k > 1 or (k == 1 and c == side):
+                        hop(side, k - 1, c).wait_recv()
+                        value = value + recv[side, k - 1, rows_of(c)].astype(F32)
+                    send[side, k, rows_of(c)] = value.astype(BF16)
+                    hop(side, k, c).start()
+        own = term(n)
+        for c in range(2):
+            total = own[c * rows_a : (c + 1) * rows_a]
             for side in range(2):
-                steps = half if side == 0 else half - 1
-                if k >= steps:
-                    continue
-                target = blk(half - k) if side == 0 else blk(k - (half - 1))
-                value = term(target)
-                if k > 0:
-                    hop(side, k - 1).wait_recv()
-                    value = value + recv[side, k - 1].astype(F32)
-                if True:
-                    send[side, k] = value.astype(BF16)
-                hop(side, k).start()
-        total = term(n)
+                hop(side, half - 1, c).wait_recv()
+                total = total + recv[side, half - 1, rows_of(c)].astype(F32)
+            on_half(c, total)
         for side in range(2):
-            steps = half if side == 0 else half - 1
-            if steps > 0:
-                hop(side, steps - 1).wait_recv()
-                total = total + recv[side, steps - 1].astype(F32)
+            for k in range(half):
+                for c in range(2):
+                    if k > 0 or c == side:
+                        hop(side, k, c).wait_send()
+
+    def narrow_hop(l, which, buffer, side, k, c, block):
+        return remote(
+            buffer.at[block, rows_of(c)],
+            buffer.at[block, rows_of(c)],
+            agz_send.at[l, which, side, k, c],
+            agz_recv.at[l, which, side, k, c],
+            {"narrow": right if side == 0 else left},
+        )
+
+    def gather_narrow_start(l, which, buffer, c):
         for side in range(2):
-            steps = half if side == 0 else half - 1
-            for k in range(steps):
-                hop(side, k).wait_send()
-        return total
+            narrow_hop(l, which, buffer, side, 0, c, n).start()
 
     def gather_narrow(l, which, buffer, on_block):
-        def hop(side, k, block):
-            return remote(
-                buffer.at[block],
-                buffer.at[block],
-                agz_send.at[l, which, side, k],
-                agz_recv.at[l, which, side, k],
-                {"narrow": right if side == 0 else left},
-            )
-
-        hop(0, 0, n).start()
-        if half > 1:
-            hop(1, 0, n).start()
+        hop = functools.partial(narrow_hop, l, which, buffer)
         on_block(n)
         for k in range(half):
-            from_left = blk(-1 - k)
-            hop(0, k, from_left).wait_recv()
-            if k + 1 < half:
-                hop(0, k + 1, from_left).start()
-            if k + 1 < half:
-                from_right = blk(1 + k)
-                hop(1, k, from_right).wait_recv()
-                if k + 2 < half:
-                    hop(1, k + 1, from_right).start()
-            on_block(from_left)
-            if k + 1 < half:
-                on_block(from_right)
-        for k in range(half):
-            hop(0, k, n).wait_send()
-            if k + 1 < half:
-                hop(1, k, n).wait_send()
+            blocks = (blk(-1 - k), blk(1 + k))
+            for stage in range(2):
+                for side in range(2):
+                    c = side if stage == 0 else 1 - side
+                    if k == half - 1 and c != side:
+                        continue
+                    hop(side, k, c, blocks[side]).wait_recv()
+                    if k + 1 < half - 1 or (k + 1 == half - 1 and c == side):
+                        hop(side, k + 1, c, blocks[side]).start()
+            on_block(blocks[0])
+            if k < half - 1:
+                on_block(blocks[1])
+        for side in range(2):
+            for k in range(half):
+                for c in range(2):
+                    if k < half - 1 or c == side:
+                        hop(side, k, c, n).wait_send()
 
     def scatter_wide(l, which, weight, values):
         def on_block(m):
@@ -334,7 +345,11 @@
         first_gate = row_table(l, 0, 2)
         drain(wq.at[l], w_sem.at[1, l])
         gather_wide_done(l, 0)
-        qkv = scatter_narrow(l, 0, wq, rs_send_q.at[l], rs_recv_q.at[l])
+        halves = []
+        scatter_narrow(
+            l, 0, wq, rs_send_q.at[l], rs_recv_q.at[l], lambda c, value: halves.append(value)
+        )
+        qkv = jnp.concatenate(halves, axis=0)
         gains = (tab[l, 24:25, 0:128], tab[l, 25:26, 0:128])
         cosine = rope[0]
         sine = rope[1]
@@ -359,6 +374,8 @@
             kv[l, sec, n, :, h * 128 : (h + 1) * 128] = jnp.where(
                 low, pltpu.roll(turned, 64, 1), upper
             ).astype(BF16)
+        for c in range(2):
+            gather_narrow_start(l, 0, kv.at[l, sec], c)
         send_result(l, 0, kv.at[l, sec, n], nc_ref)
 
         def to_sister(m):
@@ -407,6 +424,8 @@
                     weights.astype(BF16), pairs_h, preferred_element_type=F32
                 )
             att[l, n, :, h * 64 : (h + 1) * 64] = (mixed / total)[:, 64:128].astype(BF16)
+        for c in range(2):
+            gather_narrow_start(l, 1, att.at[l], c)
         drain(wo.at[l], w_sem.at[2, l])
         gather_narrow(l, 1, att.at[l], scatter_wide(l, 0, wo, att.at[l]))
         after = x_in + first_gate * scatter_wide_done(l, 0)
@@ -414,8 +433,12 @@
         second_gate = row_table(l, 1, 2)
         drain(wu.at[l], w_sem.at[3, l])
         gather_wide_done(l, 1)
-        up = scatter_narrow(l, 1, wu, rs_send_u.at[l], rs_recv_u.at[l])
-        act[l, n] = jax.nn.gelu(up, approximate=True).astype(BF16)
+
+        def activate(c, value):
+            act[l, n, rows_of(c)] = jax.nn.gelu(value, approximate=True).astype(BF16)
+            gather_narrow_start(l, 2, act.at[l], c)
+
+        scatter_narrow(l, 1, wu, rs_send_u.at[l], rs_recv_u.at[l], activate)
         drain(wd.at[l], w_sem.at[4, l])
         gather_narrow(l, 2, act.at[l], scatter_wide(l, 1, wd, act.at[l]))
         result = (after + second_gate * scatter_wide_done(l, 1)).astype(BF16)
@@ -539,10 +562,10 @@
             dma((2, 2, 2)),
             dma((2, 2, 2)),
             dma((2, 2, 2)),
-            dma((2, 2, 2, half)),
-            dma((2, 2, 2, half)),
-            dma((2, 3, 2, half)),
-            dma((2, 3, 2, half)),
+            dma((2, 2, 2, half, 2)),
+            dma((2, 2, 2, half, 2)),
+            dma((2, 3, 2, half, 2)),
+            dma((2, 3, 2, half, 2)),
             dma((2,)),
             dma((2,)),
             dma((2,)),

time: 336 us -> 301 us (0.90)
  Pallas kernels: 318 us -> 283 us
    pallas_call x1, Pallas kernels: 318 us -> 283 us  [per_device(): pl.pallas_call(functools.partial(two_layers, nw, nn), out_shape=(jax.Shap...]
where the time goes in v2:
time: 301 us
  Pallas kernels  283 us (94%)
  local copies, waits for them, and re-layouts  8.97 us (3%)
  other arithmetic  5.24 us (2%)
  matrix products  3.04 us (1%)
    pallas_call x1, Pallas kernels, per_device(): pl.pallas_call(functools.partial(two_layers, nw, nn), out_shape=(jax.Shap...  283 us

profile of v2, /device:TPU:17, one launch (start us, length us, event | category | flops | bytes accessed | tf_op | source)
XLA Modules:
  0.0 301.0 jit_solution(6946840372855536021)
XLA Ops:
  0.7 0.8 dynamic-slice_bitcast_fusion.1
  1.5 0.7 convert_element_type.38
  2.2 0.8 dynamic-slice_bitcast_fusion
  2.9 0.8 fusion.15
  3.8 0.8 slice_bitcast_fusion.3
  4.6 0.1 multiply_cosine_fusion
  4.8 1.3 and_select_fusion.kreq
  6.1 0.1 fusion.7
  6.2 0.1 fusion.9
  6.3 0.7 copy.31.kinda
  7.1 0.1 copy.23
  7.3 0.1 copy.24
  7.4 0.7 pad_maximum_fusion.rope
  8.0 3.0 %fusion.2 = f32[2,2,6,384]{3,1,2,0:T(2,128)S(1)} fusion(bf16[1,2,512,6,384]{4,2,3,1,0:T(8,128)(2,1)} %param.19, f32[2,256]{1,0:T(2,128)S(1)} %get-tuple-element.20, f32[2,256]{1,0:T(2,128)S(1)} %get-tuple-element.19), kind=kOutput, calls=%fused_computation.2 | convolution fusion | flops 9443328 | bytes 4759552 | tf_op jit(solution)/shard_map/re,kesd->krsd/dot_general | solution.py:498
  11.1 0.6 pad_maximum_fusion.1.tab_in
  11.7 0.1 copy.25
  11.9 0.7 add_select_fusion.qreq
  12.5 0.2 copy.29
  12.7 0.8 copy.32.stale
  13.5 1.0 copy.30
  14.5 283.0 %shard_map.122 = (bf16[2,64,384]{2,1,0:T(8,128)(2,1)}, bf16[2,128,384]{2,1,0:T(8,128)(2,1)}) custom-call(bf16[2,64,384]{2,1,0:T(8,128)(2,1)} %hid.1, f32[32,384]{1,0:T(8,128)} %pad_maximum_fusion.1.tab_in, f32[2,128,128]{2,1,0:T(8,128)} %pad_maximum_fusion.rope, s32[64,1]{1,0:T(8,128)} %copy.31.kinda, s32[128,1]{1,0:T(8,128)} %add_select_fusion.qreq, ...), custom_call_target="tpu_custom_call" | custom-call | tf_op jit(solution)/shard_map/pallas_call | solution.py:533
  297.5 1.1 copy.33
  298.6 0.8 copy.34
  299.4 1.5 copy.37
  (17 shorter events, 0.3 us)
Async XLA Ops:
  0.6 12.9 %copy-start = (bf16[1,384,576]{1,2,0:T(8,128)(2,1)S(1)}, bf16[1,384,576]{1,2,0:T(8,128)(2,1)}, u32[]{:S(2)}) copy-start(bf16[1,384,576]{1,2,0:T(8,128)(2,1)} %param.16) | copy-start | bytes 1327108
  0.6 11.9 %copy-start.1 = (bf16[1,2,128,3,128]{4,2,3,1,0:T(8,128)(2,1)S(1)}, bf16[1,2,128,3,128]{4,2,3,1,0:T(8,128)(2,1)}, u32[]{:S(2)}) copy-start(bf16[1,2,128,3,128]{4,2,3,1,0:T(8,128)(2,1)} %param.15) | copy-start | bytes 589828

commit v3 on v1

v3 whole, which is shorter than its diff:
```python
import functools

import jax
import jax.numpy as jnp
import numpy as np
from jax import lax
from jax.experimental import pallas as pl
from jax.experimental.pallas import tpu as pltpu
from jax.sharding import PartitionSpec as P

EPS_ROW = 1e-05
EPS_HEAD = 1e-06
NEG_FILL = -1e30
LEAD = (0, 0, 0)
F32 = jnp.float32
BF16 = jnp.bfloat16


def time_features(timesteps, feature_count):
    half_count = feature_count // 2
    frequency = jnp.exp(-jnp.log(10000.0) * jnp.arange(half_count, dtype=F32) / half_count)
    angle = timesteps.astype(F32)[:, None] * frequency[None, :]
    return jnp.concatenate([jnp.cos(angle), jnp.sin(angle)], axis=1)


def rotary_frequencies(head_dim):
    dim_frame = head_dim // 4
    dim_plane = head_dim // 8 * 3
    table = np.zeros((8, 2 * head_dim), np.float32)
    start = 0
    for axis_pos, span_dims in ((0, dim_frame), (1, dim_plane), (2, dim_plane)):
        place = np.arange(0, span_dims, 2, dtype=np.float32) / np.float32(span_dims)
        frequency = np.repeat(np.float32(10000.0) ** (-place), 2)
        for base in (0, head_dim):
            table[axis_pos, base + start : base + start + span_dims] = frequency
        start += span_dims
    return table


def two_layers(
    nw,
    nn,
    hid,
    row_kind,
    positions,
    freq,
    steps_act,
    norms,
    ada_in,
    stale,
    wq_in,
    wo_in,
    wu_in,
    wd_in,
    lo_ref,
    nc_ref,
    rope,
    ada,
    tab,
    wq,
    wo,
    wu,
    wd,
    stat_own,
    stat_all,
    entry,
    kv,
    att,
    act,
    part_out,
    part_in,
    rs_send_q,
    rs_recv_q,
    rs_send_u,
    rs_recv_u,
    terms_q,
    terms_u,
    query,
    result_buf,
    ada_sem,
    tab_sem,
    tab_send,
    w_sem,
    w_send,
    stat_sem,
    agw_sem,
    rsw_sem,
    rsz_send,
    rsz_recv,
    agz_send,
    agz_recv,
    stale_sem,
    stale_send,
    sis_sem,
    sis_send,
    out_sem,
    out_send,
):
    sec = lax.axis_index("section")
    w = lax.axis_index("wide")
    n = lax.axis_index("narrow")
    _, rows_a, feat = hid.shape
    rows_b = rope.shape[1]
    per_block = rows_b // rows_a
    rows_s = rows_a // 2
    rows_z = per_block * rows_s
    heads = kv.shape[3]
    width = feat * nn
    half = nn // 2
    other = 1 - sec
    right = lax.rem(n + 1, nn)
    left = lax.rem(n + nn - 1, nn)

    def blk(offset):
        return lax.rem(n + offset + 2 * nn, nn)

    def remote(src, dst, send_sem, recv_sem, where):
        return pltpu.make_async_remote_copy(
            src_ref=src,
            dst_ref=dst,
            send_sem=send_sem,
            recv_sem=recv_sem,
            device_id=where,
            device_id_type=pl.DeviceIdType.MESH,
        )

    def drain(ref, sem):
        pltpu.make_async_copy(ref, ref, sem).wait()

    barrier = pltpu.get_barrier_semaphore()
    for j in range(1, nw):
        pl.semaphore_signal(barrier, inc=1, device_id={"wide": lax.rem(w + j, nw)})
    for j in range(1, nn):
        pl.semaphore_signal(barrier, inc=1, device_id={"narrow": blk(j)})
    for j in range(nn):
        pl.semaphore_signal(barrier, inc=1, device_id={"section": other, "narrow": blk(j)})
    for k in range(2):
        pltpu.make_async_copy(ada_in.at[k], ada.at[k], ada_sem.at[k]).start()
    pl.semaphore_wait(barrier, nw - 1 + nn - 1 + nn)

    pairs = ((wq_in, wq), (wo_in, wo), (wu_in, wu), (wd_in, wd))

    def send_weights():
        for i, (source, held) in enumerate(pairs):
            pltpu.make_async_copy(source, held.at[sec], w_sem.at[i, sec]).start()
            remote(
                source, held.at[sec], w_send.at[i], w_sem.at[i, sec], {"section": other}
            ).start()

    lanes = lax.broadcasted_iota(jnp.int32, (rows_z, 128), 1)
    low = lanes < 64
    even = lax.rem(lanes, 2) == 0
    own_rows = pl.ds(pl.multiple_of(n * rows_b, 128), rows_b)
    own_block = pl.ds(pl.multiple_of(lax.div(w, 2) * 128, 128), 128)

    def own_patch(two_rows):
        return jnp.where(sec == 0, two_rows[0:1], two_rows[1:2])

    lines = [own_patch(positions[a, :, own_rows]) for a in range(3)]
    lines.append(own_patch(row_kind[:, own_rows]))
    lines.append(own_patch(row_kind[:, own_block]))
    lines = jnp.concatenate(lines, axis=0).astype(F32)
    columns = jnp.concatenate([lines, jnp.zeros((123, 128), F32)], axis=0).T
    odd = lax.rem(w, 2) == 1
    kind_col = jnp.where(odd, columns[rows_a : 2 * rows_a, 4:5], columns[0:rows_a, 4:5])

    def stream_rows(values, s):
        return jnp.concatenate(
            [
                values[i * rows_a + s * rows_s : i * rows_a + (s + 1) * rows_s]
                for i in range(per_block)
            ],
            axis=0,
        )

    def modulation():
        for k in range(2):
            pltpu.make_async_copy(ada_in.at[k], ada.at[k], ada_sem.at[k]).wait()
            for j in range(6):
                mixed = jnp.dot(steps_act[...], ada[k, j], preferred_element_type=F32)
                for r in range(2):
                    tab[sec, k, r * 6 + j : r * 6 + j + 1, :] = mixed[r : r + 1]
            for i in range(2):
                tab[sec, k, 12 + i : 13 + i, 0:128] = jnp.concatenate(
                    [norms[i : i + 1, :], norms[2 + i : 3 + i, :]], axis=1
                )
            remote(
                tab.at[sec, k],
                tab.at[sec, k],
                tab_send.at[k],
                tab_sem.at[k],
                {"section": other},
            ).start()

    def table_arrives(k):
        drain(tab.at[0, k], tab_sem.at[k])

    def rotations():
        angle = (
            columns[:, 0:1] * freq[0:1, :]
            + columns[:, 1:2] * freq[1:2, :]
            + columns[:, 2:3] * freq[2:3, :]
        )
        place = lax.broadcasted_iota(jnp.int32, (rows_b, 128), 1)
        sign = jnp.where(lax.rem(place, 2) == 0, -1.0, 1.0)
        rope[0] = jnp.cos(angle)
        rope[1] = sign * jnp.sin(angle)

    def row_table(l, k, s, j):
        kinds = kind_col[s * rows_s : (s + 1) * rows_s]
        out = jnp.zeros((rows_s, feat), F32)
        for kind in range(4):
            value = tab[l, k, 3 * kind + j : 3 * kind + j + 1, :]
            out = jnp.where(kinds == kind, value, out)
        return out

    def share_moments(l, k, s, x):
        total = jnp.sum(x, axis=1, keepdims=True)
        square = jnp.sum(x * x, axis=1, keepdims=True)
        place = lax.broadcasted_iota(jnp.int32, (rows_s, 128), 1)
        packed = jnp.where(place == 0, total, jnp.where(place == 1, square, 0.0))
        packed = jnp.concatenate([packed, jnp.zeros((128 - rows_s, 128), F32)], axis=0)
        turned = packed.T[0:8, :]
        stat_own[l, k, s] = turned
        for j in range(1, nn):
            remote(
                stat_own.at[l, k, s],
                stat_all.at[l, k, s, n],
                stat_sem.at[l, k, s, 0],
                stat_sem.at[l, k, s, 1],
                {"narrow": blk(j)},
            ).start()
        stat_all[l, k, s, n] = turned

    def gather_wide(l, k, s, x):
        scale = 1.0 + row_table(l, k, s, 1)
        shift = row_table(l, k, s, 0)
        others = stat_all.at[l, k, s, pl.ds(0, nn - 1)]
        drain(others, stat_sem.at[l, k, s, 1])
        summed = stat_all[l, k, s, 0]
        for j in range(1, nn):
            summed = summed + stat_all[l, k, s, j]
        back = jnp.concatenate([summed, jnp.zeros((120, 128), F32)], axis=0).T
        row_mean = back[0:rows_s, 0:1] / width
        variance = back[0:rows_s, 1:2] / width - row_mean * row_mean
        normed = (x - row_mean) * lax.rsqrt(variance + EPS_ROW)
        entry[l, k, s, w] = (normed * scale + shift).astype(BF16)
        for j in range(1, nw):
            remote(
                entry.at[l, k, s, w],
                entry.at[l, k, s, w],
                agw_sem.at[l, k, s, 0],
                agw_sem.at[l, k, s, 1],
                {"wide": lax.rem(w + j, nw)},
            ).start()
        drain(others, stat_sem.at[l, k, s, 0])

    def gather_wide_done(l, k, s):
        many = entry.at[l, k, s, pl.ds(0, nw - 1)]
        drain(many, agw_sem.at[l, k, s, 1])
        drain(many, agw_sem.at[l, k, s, 0])

    def scatter_narrow(l, norm, s, weight, depth_dim, terms, send, recv):
        far, near = s, 1 - s

        def product(rows):
            return lax.dot_general(
                rows, weight[l], (((1,), (depth_dim,)), ((), ())), preferred_element_type=F32
            )

        def term(m):
            blocks = entry[l, norm, s, pl.ds(m * per_block, per_block)]
            return product(blocks.reshape(rows_z, feat))

        def goal(side, k):
            return blk(half - k) if side == 0 else blk(k - half)

        def hop(side, k):
            return remote(
                send.at[l, s, side, k],
                recv.at[l, s, side, k],
                rsz_send.at[l, norm, s, side, k],
                rsz_recv.at[l, norm, s, side, k],
                {"narrow": right if side == 0 else left},
            )

        def put(side, k, value):
            send[l, s, side, k] = value.astype(BF16)
            hop(side, k).start()

        put(far, 0, term(goal(far, 0)))
        put(near, 1, term(goal(near, 1)))
        terms[s] = product(entry[l, norm, s].reshape(nw * rows_s, feat)).reshape(terms.shape[1:])
        for k in range(1, half):
            yield
            for side in (far, near):
                if side == near and k == 1:
                    continue
                hop(side, k - 1).wait_recv()
                put(side, k, terms[s, goal(side, k)] + recv[l, s, side, k - 1].astype(F32))
        yield
        total = terms[s, n]
        for side in (far, near):
            hop(side, half - 1).wait_recv()
            total = total + recv[l, s, side, half - 1].astype(F32)
        for side in (far, near):
            for k in range(0 if side == far else 1, half):
                hop(side, k).wait_send()
        return total

    def narrow_hop(l, which, s, view, side, k, block):
        return remote(
            view(block),
            view(block),
            agz_send.at[l, which, s, side, k],
            agz_recv.at[l, which, s, side, k],
            {"narrow": right if side == 0 else left},
        )

    def gather_narrow(l, which, s, view, on_blocks):
        far, near = s, 1 - s
        hop = functools.partial(narrow_hop, l, which, s, view)
        for side in (far, near):
            hop(side, 0, n).start()
        on_blocks([n])
        for k in range(half):
            yield
            blocks = []
            for side in (far, near):
                last = half - 1 if side == far else half - 2
                if k > last:
                    continue
                block = blk(-1 - k) if side == 0 else blk(1 + k)
                blocks.append(block)
                hop(side, k, block).wait_recv()
                if k < last:
                    hop(side, k + 1, block).start()
            on_blocks(blocks)
        for side in (far, near):
            for k in range(half if side == far else half - 1):
                hop(side, k, n).wait_send()

    def scatter_wide(l, which, s, weight, values):
        def on_blocks(blocks):
            rows = jnp.concatenate([values[l, s, m] for m in blocks], axis=0)
            sums = jnp.dot(rows, weight[l], preferred_element_type=F32).astype(BF16)
            for place, m in enumerate(blocks):
                for i in range(per_block):
                    target = m * per_block + i
                    start = place * rows_z + i * rows_s
                    piece = sums[start : start + rows_s]

                    @pl.when(target == w)
                    def _():
                        part_in[l, which, s, w] = piece

                    @pl.when(target != w)
                    def _():
                        part_out[l, which, s, target] = piece
                        remote(
                            part_out.at[l, which, s, target],
                            part_in.at[l, which, s, w],
                            rsw_sem.at[l, which, s, 0],
                            rsw_sem.at[l, which, s, 1],
                            {"wide": target},
                        ).start()

        return on_blocks

    def scatter_wide_done(l, which, s):
        many = part_in.at[l, which, s, pl.ds(0, nw - 1)]
        drain(many, rsw_sem.at[l, which, s, 1])
        total = part_in[l, which, s, 0].astype(F32)
        for j in range(1, nw):
            total = total + part_in[l, which, s, j].astype(F32)
        drain(many, rsw_sem.at[l, which, s, 0])
        return total

    def send_stale(l):
        @pl.when(sec == l)
        def _():
            for j in range(nn):
                if l == 0 and j == 0:
                    pltpu.make_async_copy(
                        stale.at[1], kv.at[l, 1, n], stale_sem.at[l]
                    ).start()
                else:
                    remote(
                        stale.at[1],
                        kv.at[l, 1, n],
                        stale_send.at[l],
                        stale_sem.at[l],
                        {"section": 0, "narrow": blk(j)},
                    ).start()

    def send_result(l, kind, s, source, target):
        @pl.when(sec == l)
        def _():
            pltpu.make_async_copy(source, target, out_sem.at[l, kind, s, sec]).start()

        @pl.when(sec != l)
        def _():
            remote(
                source,
                target,
                out_send.at[l, kind, s],
                out_sem.at[l, kind, s, sec],
                {"section": other},
            ).start()

    def half_mean(values):
        first = jnp.sum(jnp.where(low, values, 0.0), axis=1, keepdims=True)
        second = jnp.sum(jnp.where(low, 0.0, values), axis=1, keepdims=True)
        return jnp.where(low, first, second) * (1.0 / 64)

    def to_attention(l, s, x):
        gather_wide(l, 0, s, x)
        if l == 0 and s == 0:
            send_stale(0)
            rotations()
        yield
        if s == 0:
            drain(wq.at[l], w_sem.at[0, l])
        gather_wide_done(l, 0, s)
        qkv = yield from scatter_narrow(l, 0, s, wq, 1, terms_q, rs_send_q, rs_recv_q)
        gain = tab[l, 0, 12:13, 0:128]
        bias = tab[l, 0, 13:14, 0:128]
        cosine = stream_rows(rope[0], s)
        sine = stream_rows(rope[1], s)
        for h in range(heads):
            both = qkv[:, h * 192 : h * 192 + 128]
            upper = qkv[:, h * 192 + 64 : h * 192 + 192]
            center = both - half_mean(both)
            spread = half_mean(center * center)
            normed = center * lax.rsqrt(spread + EPS_HEAD) * gain + bias
            swapped = jnp.where(even, pltpu.roll(normed, 127, 1), pltpu.roll(normed, 1, 1))
            turned = normed * cosine + swapped * sine
            query[s, h] = jnp.where(low, turned * 0.125, 0.0).astype(BF16)
            fresh = jnp.where(low, pltpu.roll(turned, 64, 1), upper).astype(BF16)
            for i in range(per_block):
                kv[l, sec, n, h, i, s] = fresh[i * rows_s : (i + 1) * rows_s]

        def to_sister(blocks):
            for m in blocks:

                @pl.when(sec == 0)
                def _():
                    remote(
                        kv.at[l, 0, m, :, :, s],
                        kv.at[l, 0, m, :, :, s],
                        sis_send.at[l],
                        sis_sem.at[l],
                        {"section": 1},
                    ).start()

        send_result(l, 0, s, kv.at[l, sec, n, :, :, s], nc_ref.at[sec, :, :, s])
        yield from gather_narrow(
            l, 0, s, lambda m: kv.at[l, sec, m, :, :, s], to_sister
        )

    def attention(l):
        if l == 0:
            send_stale(1)

        @pl.when(sec == 0)
        def _():
            drain(kv.at[l, 1], stale_sem.at[l])

        @pl.when(sec == 1)
        def _():
            drain(kv.at[l, 0], sis_sem.at[l])

        requests = (columns[:, 3:4] > 1.5).astype(F32)
        request = jnp.concatenate([stream_rows(requests, s) for s in range(2)], axis=0) > 0.5
        request = request.astype(jnp.int32)
        for h in range(heads):
            queries = query[:, h].reshape(rows_b, 128)
            tops = []
            scores = []
            for p in range(2):
                pairs_h = kv[l, p, :, h].reshape(nn * rows_b, 128)
                raw = lax.dot_general(
                    queries, pairs_h, (((1,), (1,)), ((), ())), preferred_element_type=F32
                )
                key_request = lax.shift_right_logical(row_kind[p : p + 1, :], 1)
                raw = jnp.where(request == key_request, raw, NEG_FILL)
                scores.append(raw)
                tops.append(jnp.max(raw, axis=1, keepdims=True))
            top = jnp.maximum(tops[0], tops[1])
            total = jnp.zeros((rows_b, 1), F32)
            mixed = jnp.zeros((rows_b, 128), F32)
            for p in range(2):
                pairs_h = kv[l, p, :, h].reshape(nn * rows_b, 128)
                weights = jnp.exp(scores[p] - top)
                total = total + jnp.sum(weights, axis=1, keepdims=True)
                mixed = mixed + jnp.dot(
                    weights.astype(BF16), pairs_h, preferred_element_type=F32
                )
            done = (mixed / total)[:, 64:128].astype(BF16)
            for s in range(2):
                att[l, s, n, :, h * 64 : (h + 1) * 64] = done[s * rows_z : (s + 1) * rows_z]

    def from_attention(l, s, x):
        if s == 0:
            drain(wo.at[l], w_sem.at[1, l])
        yield from gather_narrow(
            l, 1, s, lambda m: att.at[l, s, m], scatter_wide(l, 0, s, wo, att)
        )
        yield
        after = x + row_table(l, 0, s, 2) * scatter_wide_done(l, 0, s)
        share_moments(l, 1, s, after)
        yield
        gather_wide(l, 1, s, after)
        yield
        if s == 0:
            drain(wu.at[l], w_sem.at[2, l])
        gather_wide_done(l, 1, s)
        up = yield from scatter_narrow(l, 1, s, wu, 0, terms_u, rs_send_u, rs_recv_u)
        act[l, s, n] = jax.nn.gelu(up, approximate=True).astype(BF16)
        if s == 0:
            drain(wd.at[l], w_sem.at[3, l])
        yield from gather_narrow(
            l, 2, s, lambda m: act.at[l, s, m], scatter_wide(l, 1, s, wd, act)
        )
        yield
        second = row_table(l, 1, s, 2) * scatter_wide_done(l, 1, s)
        result = (after + second).astype(BF16)
        result_buf[l, s] = result
        send_result(l, 1, s, result_buf.at[l, s], lo_ref.at[sec, s])
        return result.astype(F32)

    def between(s, x):
        x = yield from from_attention(0, s, x)
        share_moments(1, 0, s, x)
        inputs[s] = x
        yield
        yield from to_attention(1, s, x)

    def run(streams, lead):
        streams = list(streams)
        for _ in range(lead):
            next(streams[0], None)
        while streams:
            for stream in list(streams):
                try:
                    next(stream)
                except StopIteration:
                    streams.remove(stream)

    inputs = [hid[sec, s * rows_s : (s + 1) * rows_s].astype(F32) for s in range(2)]
    for s in range(2):
        share_moments(0, 0, s, inputs[s])
    send_weights()
    modulation()
    table_arrives(0)
    run((to_attention(0, s, inputs[s]) for s in range(2)), LEAD[0])
    attention(0)
    table_arrives(1)
    run((between(s, inputs[s]) for s in range(2)), LEAD[1])
    attention(1)
    run((from_attention(1, s, inputs[s]) for s in range(2)), LEAD[2])

    for i, (source, held) in enumerate(pairs):
        drain(held.at[0], w_send.at[i])
    for k in range(2):
        drain(tab.at[0, k], tab_send.at[k])
    for l in range(2):
        for s in range(2):

            @pl.when(sec == l)
            def _():
                for p in range(2):
                    drain(nc_ref.at[p, :, :, s], out_sem.at[l, 0, s, p])
                    drain(lo_ref.at[p, s], out_sem.at[l, 1, s, p])

            @pl.when(sec != l)
            def _():
                drain(nc_ref.at[0, :, :, s], out_send.at[l, 0, s])
                drain(lo_ref.at[0, s], out_send.at[l, 1, s])

        @pl.when(sec == l)
        def _():
            drain(kv.at[l, 1, pl.ds(0, nn - 1 + l)], stale_send.at[l])

        @pl.when(sec == 0)
        def _():
            drain(kv.at[l, 0], sis_send.at[l])


def per_device(
    hidden_in,
    row_kind,
    positions,
    timesteps,
    stale_cache,
    w_qkv,
    qk_norm,
    w_out,
    ada_weight,
    w_up,
    w_down,
):
    nw = lax.axis_size("wide")
    nn = lax.axis_size("narrow")
    _, rows_a, feat = hidden_in.shape
    rows_b = rows_a * nw // nn
    heads = stale_cache.shape[3]
    head_dim = stale_cache.shape[4] // 2
    depth = ada_weight.shape[2]
    activated = jax.nn.silu(time_features(timesteps, depth)).astype(BF16)
    activated = jnp.pad(activated, ((0, 14), (0, 0)))
    freq = jnp.asarray(rotary_frequencies(head_dim))
    rows_s = rows_a // 2
    rows_z = rows_b // 2
    per_block = rows_b // rows_a
    split = (2, heads, per_block, 2, rows_s, 2 * head_dim)
    stale = jnp.transpose(stale_cache[0], (0, 2, 1, 3)).reshape(split)
    ada = jnp.transpose(ada_weight[0], (0, 2, 1, 3))
    cols_q = w_qkv.shape[2]
    cols_u = w_up.shape[2]
    cols_o = w_out.shape[1]
    half = nn // 2
    vm = pl.BlockSpec(memory_space=pltpu.VMEM)
    anywhere = pl.BlockSpec(memory_space=pl.ANY)
    dma = pltpu.SemaphoreType.DMA
    layer_out, cache_out = pl.pallas_call(
        functools.partial(two_layers, nw, nn),
        out_shape=(
            jax.ShapeDtypeStruct((2, 2, rows_s, feat), BF16),
            jax.ShapeDtypeStruct(split, BF16),
        ),
        in_specs=[vm] * 6 + [anywhere] * 6,
        out_specs=(anywhere, anywhere),
        scratch_shapes=[
            pltpu.VMEM((2, rows_b, 2 * head_dim), F32),
            pltpu.VMEM((2, 6, depth, feat), BF16),
            pltpu.VMEM((2, 2, 16, feat), F32),
            pltpu.VMEM((2, cols_q, feat), BF16),
            pltpu.VMEM((2, cols_o, feat), BF16),
            pltpu.VMEM((2, feat, cols_u), BF16),
            pltpu.VMEM((2, cols_u, feat), BF16),
            pltpu.VMEM((2, 2, 2, 8, 128), F32),
            pltpu.VMEM((2, 2, 2, nn, 8, 128), F32),
            pltpu.VMEM((2, 2, 2, nw, rows_s, feat), BF16),
            pltpu.VMEM((2, 2, nn) + split[1:], BF16),
            pltpu.VMEM((2, 2, nn, rows_z, cols_o), BF16),
            pltpu.VMEM((2, 2, nn, rows_z, cols_u), BF16),
            pltpu.VMEM((2, 2, 2, nw, rows_s, feat), BF16),
            pltpu.VMEM((2, 2, 2, nw, rows_s, feat), BF16),
            pltpu.VMEM((2, 2, 2, half, rows_z, cols_q), BF16),
            pltpu.VMEM((2, 2, 2, half, rows_z, cols_q), BF16),
            pltpu.VMEM((2, 2, 2, half, rows_z, cols_u), BF16),
            pltpu.VMEM((2, 2, 2, half, rows_z, cols_u), BF16),
            pltpu.VMEM((2, nn, rows_z, cols_q), F32),
            pltpu.VMEM((2, nn, rows_z, cols_u), F32),
            pltpu.VMEM((2, heads, rows_z, 2 * head_dim), BF16),
            pltpu.VMEM((2, 2, rows_s, feat), BF16),
            dma((2,)),
            dma((2,)),
            dma((2,)),
            dma((4, 2)),
            dma((4,)),
            dma((2, 2, 2, 2)),
            dma((2, 2, 2, 2)),
            dma((2, 2, 2, 2)),
            dma((2, 2, 2, 2, half)),
            dma((2, 2, 2, 2, half)),
            dma((2, 3, 2, 2, half)),
            dma((2, 3, 2, 2, half)),
            dma((2,)),
            dma((2,)),
            dma((2,)),
            dma((2,)),
            dma((2, 2, 2, 2)),
            dma((2, 2, 2)),
        ],
        compiler_params=pltpu.CompilerParams(
            collective_id=0, has_side_effects=True, vmem_limit_bytes=60 * 1024 * 1024
        ),
    )(
        hidden_in,
        row_kind,
        positions,
        freq,
        activated,
        qk_norm[0],
        ada,
        stale,
        jnp.transpose(w_qkv[0]),
        w_out[0],
        w_up[0],
        w_down[0],
    )
    return (
        layer_out.reshape(1, 2, rows_a, feat),
        jnp.transpose(
            cache_out.reshape(2, heads, rows_b, 2 * head_dim), (0, 2, 1, 3)
        )[None],
    )


def solution(mesh):
    in_specs = (
        P(None, "wide", "narrow"),
        P(),
        P(),
        P(),
        P("section", None, "narrow", "wide", None),
        P("section", "narrow", "wide"),
        P("section", None, None),
        P("section", "wide", "narrow"),
        P("section", None, None, None, "narrow"),
        P("section", "narrow", "wide"),
        P("section", "wide", "narrow"),
    )
    out_specs = (P("section", None, "wide", "narrow"), P("section", None, "narrow", "wide", None))
    return jax.shard_map(
        per_device, mesh=mesh, in_specs=in_specs, out_specs=out_specs, check_vma=False
    )
```

time: 336 us -> 278 us (0.83)
  Pallas kernels: 318 us -> 272 us
  local copies, waits for them, and re-layouts: 8.97 us -> 3.77 us
  other arithmetic: 5.24 us -> 0.8 us
    pallas_call x1, Pallas kernels: 318 us -> 272 us  [per_device(): pl.pallas_call(functools.partial(two_layers, nw, nn), out_shape=(jax.Shap...]
where the time goes in v3:
time: 278 us
  Pallas kernels  272 us (98%)
  local copies, waits for them, and re-layouts  3.77 us (1%)
    pallas_call x1, Pallas kernels, per_device(): pl.pallas_call(functools.partial(two_layers, nw, nn), out_shape=(jax.Shap...  272 us

profile of v3, /device:TPU:17, one launch (start us, length us, event | category | flops | bytes accessed | tf_op | source)
XLA Modules:
  0.0 277.6 jit_solution(11314060554857238513)
XLA Ops:
  0.6 0.7 convert_element_type.8
  1.3 0.1 multiply_cosine_fusion
  1.4 0.6 pad.4.steps_act
  2.1 272.4 %shard_map.131 = (bf16[2,2,32,384]{3,2,1,0:T(8,128)(2,1)}, bf16[2,3,2,2,32,128]{5,4,3,2,1,0:T(8,128)(2,1)}) custom-call(bf16[2,64,384]{2,1,0:T(8,128)(2,1)} %hid.1, s32[2,1024]{1,0:T(2,128)} %row_kind.1, s32[3,2,1024]{2,1,0:T(2,128)} %positions.1, f32[8,128]{1,0:T(8,128)} %constant.13.clone.freq, bf16[16,512]{1,0:T(8,128)(2,1)} %pad.4.steps_act, ...), custom_call_target="tpu_custom_call" | custom-call | tf_op jit(solution)/shard_map/pallas_call | solution.py:626
  274.5 1.5 copy.16
  276.0 1.6 copy.17
  (2 shorter events, 0.0 us)

commit v4 on v3

--- a/solution.py
+++ b/solution.py
@@ -11,7 +11,6 @@
 EPS_ROW = 1e-05
 EPS_HEAD = 1e-06
 NEG_FILL = -1e30
-LEAD = (0, 0, 0)
 F32 = jnp.float32
 BF16 = jnp.bfloat16
 
@@ -95,6 +94,7 @@
     sis_send,
     out_sem,
     out_send,
+    turn,
 ):
     sec = lax.axis_index("section")
     w = lax.axis_index("wide")
@@ -414,6 +414,12 @@
         return jnp.where(low, first, second) * (1.0 / 64)
 
     def to_attention(l, s, x):
+        if l == 0 and s == 0:
+
+            @pl.when(sec == 1)
+            def _():
+                pl.semaphore_wait(turn, 1)
+
         gather_wide(l, 0, s, x)
         if l == 0 and s == 0:
             send_stale(0)
@@ -423,6 +429,12 @@
             drain(wq.at[l], w_sem.at[0, l])
         gather_wide_done(l, 0, s)
         qkv = yield from scatter_narrow(l, 0, s, wq, 1, terms_q, rs_send_q, rs_recv_q)
+        if l == 0 and s == 1:
+
+            @pl.when(sec == 0)
+            def _():
+                pl.semaphore_signal(turn, inc=1, device_id={"section": 1})
+
         gain = tab[l, 0, 12:13, 0:128]
         bias = tab[l, 0, 13:14, 0:128]
         cosine = stream_rows(rope[0], s)
@@ -536,10 +548,7 @@
         yield
         yield from to_attention(1, s, x)
 
-    def run(streams, lead):
-        streams = list(streams)
-        for _ in range(lead):
-            next(streams[0], None)
+    def run(streams):
         while streams:
             for stream in list(streams):
                 try:
@@ -553,12 +562,12 @@
     send_weights()
     modulation()
     table_arrives(0)
-    run((to_attention(0, s, inputs[s]) for s in range(2)), LEAD[0])
+    run([to_attention(0, s, inputs[s]) for s in range(2)])
     attention(0)
     table_arrives(1)
-    run((between(s, inputs[s]) for s in range(2)), LEAD[1])
+    run([between(s, inputs[s]) for s in range(2)])
     attention(1)
-    run((from_attention(1, s, inputs[s]) for s in range(2)), LEAD[2])
+    run([from_attention(1, s, inputs[s]) for s in range(2)])
 
     for i, (source, held) in enumerate(pairs):
         drain(held.at[0], w_send.at[i])
@@ -673,6 +682,7 @@
             dma((2,)),
             dma((2, 2, 2, 2)),
             dma((2, 2, 2)),
+            pltpu.SemaphoreType.REGULAR,
         ],
         compiler_params=pltpu.CompilerParams(
             collective_id=0, has_side_effects=True, vmem_limit_bytes=60 * 1024 * 1024

time: 278 us -> 270 us (0.971)
  Pallas kernels: 272 us -> 265 us
    pallas_call x1, Pallas kernels: 272 us -> 265 us  [per_device(): pl.pallas_call(functools.partial(two_layers, nw, nn), out_shape=(jax.Shap...]
where the time goes in v4:
time: 270 us
  Pallas kernels  265 us (98%)
  local copies, waits for them, and re-layouts  3.77 us (1%)
    pallas_call x1, Pallas kernels, per_device(): pl.pallas_call(functools.partial(two_layers, nw, nn), out_shape=(jax.Shap...  265 us

profile of v4, /device:TPU:17, one launch (start us, length us, event | category | flops | bytes accessed | tf_op | source)
XLA Modules:
  0.0 269.8 jit_solution(10638648515423941068)
XLA Ops:
  0.6 0.7 convert_element_type.8
  1.3 0.1 multiply_cosine_fusion
  1.4 0.6 pad.4.steps_act
  2.1 264.6 %shard_map.131 = (bf16[2,2,32,384]{3,2,1,0:T(8,128)(2,1)}, bf16[2,3,2,2,32,128]{5,4,3,2,1,0:T(8,128)(2,1)}) custom-call(bf16[2,64,384]{2,1,0:T(8,128)(2,1)} %hid.1, s32[2,1024]{1,0:T(2,128)} %row_kind.1, s32[3,2,1024]{2,1,0:T(2,128)} %positions.1, f32[8,128]{1,0:T(8,128)} %constant.13.clone.freq, bf16[16,512]{1,0:T(8,128)(2,1)} %pad.4.steps_act, ...), custom_call_target="tpu_custom_call" | custom-call | tf_op jit(solution)/shard_map/pallas_call | solution.py:635
  266.7 1.5 copy.16
  268.2 1.6 copy.17
  (2 shorter events, 0.0 us)

commit v5 on v4

--- a/solution.py
+++ b/solution.py
@@ -275,70 +275,89 @@
         def goal(side, k):
             return blk(half - k) if side == 0 else blk(k - half)
 
-        def hop(side, k):
+        def part(c):
+            return pl.ds(c * rows_s, rows_s)
+
+        def hop(side, k, c):
             return remote(
-                send.at[l, s, side, k],
-                recv.at[l, s, side, k],
-                rsz_send.at[l, norm, s, side, k],
-                rsz_recv.at[l, norm, s, side, k],
+                send.at[l, s, side, k, part(c)],
+                recv.at[l, s, side, k, part(c)],
+                rsz_send.at[l, norm, s, side, k, c],
+                rsz_recv.at[l, norm, s, side, k, c],
                 {"narrow": right if side == 0 else left},
             )
 
-        def put(side, k, value):
-            send[l, s, side, k] = value.astype(BF16)
-            hop(side, k).start()
-
-        put(far, 0, term(goal(far, 0)))
-        put(near, 1, term(goal(near, 1)))
+        def put(side, k, c, value):
+            send[l, s, side, k, part(c)] = value.astype(BF16)
+            hop(side, k, c).start()
+
+        for side, k in ((far, 0), (near, 1)):
+            first = term(goal(side, k))
+            for c in range(per_block):
+                put(side, k, c, first[c * rows_s : (c + 1) * rows_s])
         terms[s] = product(entry[l, norm, s].reshape(nw * rows_s, feat)).reshape(terms.shape[1:])
         for k in range(1, half):
             yield
-            for side in (far, near):
-                if side == near and k == 1:
-                    continue
-                hop(side, k - 1).wait_recv()
-                put(side, k, terms[s, goal(side, k)] + recv[l, s, side, k - 1].astype(F32))
+            if l == 0 and norm == 0 and s == 1 and k == half - 1:
+
+                @pl.when(sec == 0)
+                def _():
+                    pl.semaphore_signal(turn, inc=1, device_id={"section": 1})
+
+            for c in range(per_block):
+                for side in (far, near):
+                    if side == near and k == 1:
+                        continue
+                    hop(side, k - 1, c).wait_recv()
+                    own = terms[s, goal(side, k), part(c)]
+                    put(side, k, c, own + recv[l, s, side, k - 1, part(c)].astype(F32))
         yield
         total = terms[s, n]
         for side in (far, near):
-            hop(side, half - 1).wait_recv()
+            for c in range(per_block):
+                hop(side, half - 1, c).wait_recv()
             total = total + recv[l, s, side, half - 1].astype(F32)
         for side in (far, near):
             for k in range(0 if side == far else 1, half):
-                hop(side, k).wait_send()
+                for c in range(per_block):
+                    hop(side, k, c).wait_send()
         return total
 
-    def narrow_hop(l, which, s, view, side, k, block):
+    def narrow_hop(l, which, s, view, side, k, c, block):
         return remote(
-            view(block),
-            view(block),
-            agz_send.at[l, which, s, side, k],
-            agz_recv.at[l, which, s, side, k],
+            view(block, c),
+            view(block, c),
+            agz_send.at[l, which, s, side, k, c],
+            agz_recv.at[l, which, s, side, k, c],
             {"narrow": right if side == 0 else left},
         )
 
     def gather_narrow(l, which, s, view, on_blocks):
         far, near = s, 1 - s
         hop = functools.partial(narrow_hop, l, which, s, view)
-        for side in (far, near):
-            hop(side, 0, n).start()
+        for c in range(per_block):
+            for side in (far, near):
+                hop(side, 0, c, n).start()
         on_blocks([n])
         for k in range(half):
             yield
             blocks = []
-            for side in (far, near):
-                last = half - 1 if side == far else half - 2
-                if k > last:
-                    continue
-                block = blk(-1 - k) if side == 0 else blk(1 + k)
-                blocks.append(block)
-                hop(side, k, block).wait_recv()
-                if k < last:
-                    hop(side, k + 1, block).start()
+            for c in range(per_block):
+                for side in (far, near):
+                    last = half - 1 if side == far else half - 2
+                    if k > last:
+                        continue
+                    block = blk(-1 - k) if side == 0 else blk(1 + k)
+                    if c == 0:
+                        blocks.append(block)
+                    hop(side, k, c, block).wait_recv()
+                    if k < last:
+                        hop(side, k + 1, c, block).start()
             on_blocks(blocks)
         for side in (far, near):
             for k in range(half if side == far else half - 1):
-                hop(side, k, n).wait_send()
+                for c in range(per_block):
+                    hop(side, k, c, n).wait_send()
 
     def scatter_wide(l, which, s, weight, values):
         def on_blocks(blocks):
@@ -429,12 +448,6 @@
             drain(wq.at[l], w_sem.at[0, l])
         gather_wide_done(l, 0, s)
         qkv = yield from scatter_narrow(l, 0, s, wq, 1, terms_q, rs_send_q, rs_recv_q)
-        if l == 0 and s == 1:
-
-            @pl.when(sec == 0)
-            def _():
-                pl.semaphore_signal(turn, inc=1, device_id={"section": 1})
-
         gain = tab[l, 0, 12:13, 0:128]
         bias = tab[l, 0, 13:14, 0:128]
         cosine = stream_rows(rope[0], s)
@@ -467,7 +480,7 @@
 
         send_result(l, 0, s, kv.at[l, sec, n, :, :, s], nc_ref.at[sec, :, :, s])
         yield from gather_narrow(
-            l, 0, s, lambda m: kv.at[l, sec, m, :, :, s], to_sister
+            l, 0, s, lambda m, c: kv.at[l, sec, m, :, c, s], to_sister
         )
 
     def attention(l):
@@ -516,7 +529,7 @@
         if s == 0:
             drain(wo.at[l], w_sem.at[1, l])
         yield from gather_narrow(
-            l, 1, s, lambda m: att.at[l, s, m], scatter_wide(l, 0, s, wo, att)
+            l, 1, s, lambda m, c: att.at[l, s, m, pl.ds(c * rows_s, rows_s)], scatter_wide(l, 0, s, wo, att)
         )
         yield
         after = x + row_table(l, 0, s, 2) * scatter_wide_done(l, 0, s)
@@ -532,7 +545,7 @@
         if s == 0:
             drain(wd.at[l], w_sem.at[3, l])
         yield from gather_narrow(
-            l, 2, s, lambda m: act.at[l, s, m], scatter_wide(l, 1, s, wd, act)
+            l, 2, s, lambda m, c: act.at[l, s, m, pl.ds(c * rows_s, rows_s)], scatter_wide(l, 1, s, wd, act)
         )
         yield
         second = row_table(l, 1, s, 2) * scatter_wide_done(l, 1, s)
@@ -672,10 +685,10 @@
             dma((2, 2, 2, 2)),
             dma((2, 2, 2, 2)),
             dma((2, 2, 2, 2)),
-            dma((2, 2, 2, 2, half)),
-            dma((2, 2, 2, 2, half)),
-            dma((2, 3, 2, 2, half)),
-            dma((2, 3, 2, 2, half)),
+            dma((2, 2, 2, 2, half, per_block)),
+            dma((2, 2, 2, 2, half, per_block)),
+            dma((2, 3, 2, 2, half, per_block)),
+            dma((2, 3, 2, 2, half, per_block)),
             dma((2,)),
             dma((2,)),
             dma((2,)),

time: 270 us -> 263 us (0.974)
  Pallas kernels: 265 us -> 257 us
    pallas_call x1, Pallas kernels: 265 us -> 257 us  [per_device(): pl.pallas_call(functools.partial(two_layers, nw, nn), out_shape=(jax.Shap...]
where the time goes in v5:
time: 263 us
  Pallas kernels  257 us (98%)
  local copies, waits for them, and re-layouts  3.77 us (1%)
    pallas_call x1, Pallas kernels, per_device(): pl.pallas_call(functools.partial(two_layers, nw, nn), out_shape=(jax.Shap...  257 us

profile of v5, /device:TPU:17, one launch (start us, length us, event | category | flops | bytes accessed | tf_op | source)
XLA Modules:
  0.0 262.5 jit_solution(12053739578701856210)
XLA Ops:
  0.6 0.7 convert_element_type.8
  1.3 0.1 multiply_cosine_fusion
  1.4 0.6 pad.4.steps_act
  2.1 257.3 %shard_map.131 = (bf16[2,2,32,384]{3,2,1,0:T(8,128)(2,1)}, bf16[2,3,2,2,32,128]{5,4,3,2,1,0:T(8,128)(2,1)}) custom-call(bf16[2,64,384]{2,1,0:T(8,128)(2,1)} %hid.1, s32[2,1024]{1,0:T(2,128)} %row_kind.1, s32[3,2,1024]{2,1,0:T(2,128)} %positions.1, f32[8,128]{1,0:T(8,128)} %constant.13.clone.freq, bf16[16,512]{1,0:T(8,128)(2,1)} %pad.4.steps_act, ...), custom_call_target="tpu_custom_call" | custom-call | tf_op jit(solution)/shard_map/pallas_call | solution.py:648
  259.4 1.5 copy.16
  260.9 1.6 copy.17
  (2 shorter events, 0.0 us)

commit v6 on v5

--- a/solution.py
+++ b/solution.py
@@ -173,8 +173,8 @@
             axis=0,
         )
 
-    def modulation():
-        for k in range(2):
+    def modulation(norm_list):
+        for k in norm_list:
             pltpu.make_async_copy(ada_in.at[k], ada.at[k], ada_sem.at[k]).wait()
             for j in range(6):
                 mixed = jnp.dot(steps_act[...], ada[k, j], preferred_element_type=F32)
@@ -443,6 +443,7 @@
         if l == 0 and s == 0:
             send_stale(0)
             rotations()
+            modulation((1,))
         yield
         if s == 0:
             drain(wq.at[l], w_sem.at[0, l])
@@ -573,7 +574,7 @@
     for s in range(2):
         share_moments(0, 0, s, inputs[s])
     send_weights()
-    modulation()
+    modulation((0,))
     table_arrives(0)
     run([to_attention(0, s, inputs[s]) for s in range(2)])
     attention(0)

time: 263 us -> 262 us (level)
  no operation moved by 1% of the time
where the time goes in v6:
time: 262 us
  Pallas kernels  257 us (98%)
  local copies, waits for them, and re-layouts  3.77 us (1%)
    pallas_call x1, Pallas kernels, per_device(): pl.pallas_call(functools.partial(two_layers, nw, nn), out_shape=(jax.Shap...  257 us

profile of v6, /device:TPU:17, one launch (start us, length us, event | category | flops | bytes accessed | tf_op | source)
XLA Modules:
  0.0 262.2 jit_solution(2309439806033403025)
XLA Ops:
  0.6 0.7 convert_element_type.8
  1.3 0.1 multiply_cosine_fusion
  1.4 0.6 pad.4.steps_act
  2.1 257.0 %shard_map.131 = (bf16[2,2,32,384]{3,2,1,0:T(8,128)(2,1)}, bf16[2,3,2,2,32,128]{5,4,3,2,1,0:T(8,128)(2,1)}) custom-call(bf16[2,64,384]{2,1,0:T(8,128)(2,1)} %hid.1, s32[2,1024]{1,0:T(2,128)} %row_kind.1, s32[3,2,1024]{2,1,0:T(2,128)} %positions.1, f32[8,128]{1,0:T(8,128)} %constant.13.clone.freq, bf16[16,512]{1,0:T(8,128)(2,1)} %pad.4.steps_act, ...), custom_call_target="tpu_custom_call" | custom-call | tf_op jit(solution)/shard_map/pallas_call | solution.py:649
  259.0 1.5 copy.16
  260.6 1.6 copy.17
  (2 shorter events, 0.0 us)
